TPU v7x, 256 devices: a whole 4x4x8 slice. The times are simulated.
256 devices in a mesh: gx: 8 (over y, core), gy: 32 (over z, x).
Axes of the slice: x: 4, y: 4, z: 8, core: 2. Of those that a mesh axis runs over, the one named last changes fastest.
Arguments:
- right_side: float32 [256, 512, 256], P('gx', 'gy'), may hold values from -8 to 8
- coefficient: float32 [256, 512, 256], P('gx', 'gy'), may hold values from 0.1 to 10
Outputs:
- solution_field: float32 [256, 512, 256], P('gx', 'gy')
- residual: float32 [256, 512, 256], P('gx', 'gy')
All inputs are finite; a program needn't handle non-finite values.
Results may differ from a plain program's by a relative error of at most 0.0003.
Values sent between devices are 32-bit elements; how exact they have to be, the bound alone decides.
A program may use at most 128 MiB of HBM per device.

v0:
```python
from functools import partial

import jax
import jax.numpy as jnp
from jax import lax
from jax.sharding import PartitionSpec as P

LEVELS = 5
PRE = 2
POST = 2
BOTTOM = 8


SMOOTH_LO = 0.5
SMOOTH_HI = 2.0
COARSE_LO = 0.05
COARSE_HI = 2.0


def with_halo(value, sides, width):
    for axis, dim in sides:
        size, length = (lax.axis_size(axis), value.shape[dim])
        up = [(i, (i + 1) % size) for i in range(size - 1)]
        down = [(j, i) for i, j in up]
        last = lax.slice_in_dim(value, length - width, length, axis=dim)
        leading = lax.slice_in_dim(value, 0, width, axis=dim)
        before = lax.ppermute(last, axis, up)
        after = lax.ppermute(leading, axis, down)
        value = jnp.concatenate([before, value, after], axis=dim)
    return value


def harmonic(own, other):
    return 2.0 * own * other / (own + other)


def face_weights(conduct, padded):
    lower_x = jnp.where(padded[:-2, 1:-1, :] > 0.0, padded[:-2, 1:-1, :], conduct)
    upper_x = jnp.where(padded[2:, 1:-1, :] > 0.0, padded[2:, 1:-1, :], conduct)
    lower_y = jnp.where(padded[1:-1, :-2, :] > 0.0, padded[1:-1, :-2, :], conduct)
    upper_y = jnp.where(padded[1:-1, 2:, :] > 0.0, padded[1:-1, 2:, :], conduct)
    edged = jnp.pad(conduct, ((0, 0), (0, 0), (1, 1)), mode="edge")
    lower_z = edged[:, :, :-2]
    upper_z = edged[:, :, 2:]
    faces = [
        harmonic(conduct, other) for other in (lower_x, upper_x, lower_y, upper_y, lower_z, upper_z)
    ]
    total = faces[0] + faces[1] + faces[2] + faces[3] + faces[4] + faces[5]
    return tuple(faces) + (total,)


def stencil(field, padded, weights, scale):
    zpad = jnp.pad(field, ((0, 0), (0, 0), (1, 1)))
    beside = weights[0] * padded[:-2, 1:-1, :] + weights[1] * padded[2:, 1:-1, :]
    beside = beside + weights[2] * padded[1:-1, :-2, :] + weights[3] * padded[1:-1, 2:, :]
    beside = beside + weights[4] * zpad[:, :, :-2] + weights[5] * zpad[:, :, 2:]
    return scale * (weights[6] * field - beside)


def pad_plane(field):
    return jnp.pad(field, ((1, 1), (1, 1), (0, 0)))


def whole_operate(field, weights, scale):
    return stencil(field, pad_plane(field), weights, scale)


def local_operate(field, weights, scale):
    padded = with_halo(field, (("gx", 0), ("gy", 1)), 1)
    return stencil(field, padded, weights, scale)


def chebyshev(source, start, sweeps, low_end, high_end, operate, inverse):
    theta_val = (high_end + low_end) / 2.0
    half_width = (high_end - low_end) / 2.0
    sigma_val = theta_val / half_width
    rho_now = 1.0 / sigma_val
    if start is None:
        update = inverse * source / theta_val
        iterate = update
    else:
        update = inverse * (source - operate(start)) / theta_val
        iterate = start + update
    for sweep_index in range(sweeps - 1):
        rho_next = 1.0 / (2.0 * sigma_val - rho_now)
        update = rho_next * rho_now * update + 2.0 * rho_next / half_width * inverse * (
            source - operate(iterate)
        )
        iterate = iterate + update
        rho_now = rho_next
    return iterate


def restrict(field):
    size_x, size_y, size_z = field.shape
    return jnp.mean(field.reshape(size_x // 2, 2, size_y // 2, 2, size_z // 2, 2), axis=(1, 3, 5))


def prolong(field):
    size_x, size_y, size_z = field.shape
    grown = jnp.broadcast_to(field[:, None, :, None, :, None], (size_x, 2, size_y, 2, size_z, 2))
    return grown.reshape(2 * size_x, 2 * size_y, 2 * size_z)


def cycle(level_index, source, conduct):
    weights = face_weights(conduct, pad_plane(conduct))
    scale = 0.25**level_index
    inverse = 1.0 / (scale * weights[6])
    operate = partial(whole_operate, weights=weights, scale=scale)
    return chebyshev(source, None, BOTTOM, COARSE_LO, COARSE_HI, operate, inverse)


def collect(source, conduct):
    block_x, block_y, block_z = source.shape
    count_x = lax.axis_size("gx")
    count_y = lax.axis_size("gy")
    gathered = (
        lax.all_gather(source, ("gx", "gy"), axis=0, tiled=True),
        lax.all_gather(conduct, ("gx", "gy"), axis=0, tiled=True),
    )
    arranged = []
    for member in gathered:
        blocks = member.reshape(count_x, count_y, block_x, block_y, block_z)
        arranged.append(
            blocks.transpose(0, 2, 1, 3, 4).reshape(count_x * block_x, count_y * block_y, block_z)
        )
    return (arranged[0], arranged[1])


def own_block(whole, shape):
    start_x = lax.axis_index("gx") * shape[0]
    start_y = lax.axis_index("gy") * shape[1]
    return lax.dynamic_slice(whole, (start_x, start_y, jnp.zeros((), jnp.int32)), shape)


def per_device(right_side, coefficient):
    joined = LEVELS - 1
    conducts = [coefficient]
    for level_index in range(1, joined + 1):
        conducts.append(restrict(conducts[-1]))
    operators = []
    inverses = []
    for level_index in range(joined):
        padded = with_halo(conducts[level_index], (("gx", 0), ("gy", 1)), 1)
        weights = face_weights(conducts[level_index], padded)
        scale = 0.25**level_index
        inverses.append(1.0 / (scale * weights[6]))
        operators.append(partial(local_operate, weights=weights, scale=scale))
    sources = [right_side]
    smoothed = []
    for level_index in range(joined):
        operate = operators[level_index]
        iterate = chebyshev(
            sources[level_index], None, PRE, SMOOTH_LO, SMOOTH_HI, operate, inverses[level_index]
        )
        smoothed.append(iterate)
        sources.append(restrict(sources[level_index] - operate(iterate)))
    whole_source, whole_conduct = collect(sources[joined], conducts[joined])
    correction = own_block(cycle(joined, whole_source, whole_conduct), sources[joined].shape)
    for level_index in reversed(range(joined)):
        iterate = smoothed[level_index] + prolong(correction)
        correction = chebyshev(
            sources[level_index],
            iterate,
            POST,
            SMOOTH_LO,
            SMOOTH_HI,
            operators[level_index],
            inverses[level_index],
        )
    residual = right_side - operators[0](correction)
    return (correction, residual)


def solution(mesh):
    in_specs = (P("gx", "gy", None), P("gx", "gy", None))
    out_specs = (P("gx", "gy", None), P("gx", "gy", None))
    return jax.shard_map(
        per_device, mesh=mesh, in_specs=in_specs, out_specs=out_specs, check_vma=False
    )
```

profile of v0, /device:TPU:103, one launch (start us, length us, event | category | flops | bytes accessed | tf_op | source)
XLA Modules:
  0.0 702.0 jit_solution(18021534122502074643)
XLA Ops:
  7.2 35.6 %reshape.80 = f32[16,2,8,2,128,2]{5,4,3,2,1,0:T(8,128)} reshape(f32[32,16,256]{2,1,0:T(8,128)} %param.3) | data formatting | bytes 1048576 | tf_op jit(solution)/shard_map/reshape | solution.py:96
  42.8 12.2 %reduce_sum.86 = f32[16,8,128]{2,1,0:T(8,128)S(1)} reduce(f32[16,2,8,2,128,2]{5,4,3,2,1,0:T(8,128)} %reshape.80, f32[]{:T(128)} %constant.35.clone.1), dimensions={1,3,5}, to_apply=%region_0.0 | reduce | flops 114688 | bytes 589828 | tf_op jit(solution)/shard_map/reduce_sum | solution.py:96
  62.0 5.5 div.203
  70.2 4.7 collective-permute-start.2
  76.9 6.0 collective-permute-done.3
  84.8 5.1 collective-permute-start.4
  124.2 6.5 collective-permute-start.10
  134.1 35.6 %reshape.81 = f32[16,2,8,2,128,2]{5,4,3,2,1,0:T(8,128)} reshape(f32[32,16,256]{2,1,0:T(8,128)} %fusion.13) | data formatting | bytes 1048576 | tf_op jit(solution)/shard_map/reshape | solution.py:96
  169.7 12.2 %reduce_sum.87 = f32[16,8,128]{2,1,0:T(8,128)S(1)} reduce(f32[16,2,8,2,128,2]{5,4,3,2,1,0:T(8,128)} %reshape.81, f32[]{:T(128)} %constant.35.clone.1), dimensions={1,3,5}, to_apply=%region_1.0 | reduce | flops 114688 | bytes 589828 | tf_op jit(solution)/shard_map/reduce_sum | solution.py:96
  195.1 7.0 collective-permute-start.18
  205.5 4.7 collective-permute-done.19
  229.5 5.3 collective-permute-start.22
  238.6 6.3 reshape.82
  258.6 7.0 collective-permute-start.30
  267.5 59.7 %all-gather.2 = f32[256,2,16]{2,1,0:T(2,128)S(1)} all-gather(f32[1,2,16]{2,1,0:T(2,128)S(1)} %multiply_bitcast_fusion.1), channel_id=2, replica_groups=mesh['gx'=8,'gy'=32] {'gx','gy'}, dimensions={0}, use_global_device_ids=true | all-gather | bytes 32896 | tf_op jit(solution)/shard_map/all_gather | solution.py:119
  328.2 4.6 collective-permute-start.36
  343.7 6.0 collective-permute-start.34
  367.6 5.1 collective-permute-start.42
  397.4 6.0 collective-permute-done.47
  408.4 57.4 %all-gather.3 = f32[256,2,16]{2,1,0:T(2,128)S(1)} all-gather(f32[1,2,16]{2,1,0:T(2,128)S(1)} %multiply_bitcast_fusion), channel_id=3, replica_groups=mesh['gx'=8,'gy'=32] {'gx','gy'}, dimensions={0}, use_global_device_ids=true | all-gather | bytes 32896 | tf_op jit(solution)/shard_map/all_gather | solution.py:118
  489.3 5.3 collective-permute-start.50
  496.5 5.8 collective-permute-done.51
  607.1 11.4 %broadcast_in_dim.36 = f32[16,2,8,2,128,2]{5,4,3,2,1,0:T(8,128)} broadcast(f32[16,8,128]{2,1,0:T(8,128)S(1)} %fusion.220), dimensions={0,2,4} | broadcast | bytes 589824 | tf_op jit(solution)/shard_map/broadcast_in_dim | solution.py:101
  618.5 24.6 %reshape.90 = f32[32,16,256]{2,1,0:T(8,128)} reshape(f32[16,2,8,2,128,2]{5,4,3,2,1,0:T(8,128)} %broadcast_in_dim.36) | data formatting | bytes 1048576 | tf_op jit(solution)/shard_map/reshape | solution.py:102
  (337 shorter events, 360.1 us)
Async XLA Ops:
  1.4 68.7 %collective-permute-start = (f32[1,16,256]{2,1,0:T(8,128)S(1)}, f32[1,16,256]{2,1,0:T(8,128)S(1)}, u32[]{:S(2)}, u32[]{:S(2)}) collective-permute-start(f32[1,16,256]{2,1,0:T(8,128)S(1)} %get-tuple-element.81), channel_id=1, source_target_pairs={{0,32},{32,64},{64,96},{96,128},{128,160},{160,192},{192,224},{1,3... | collective-permute-start | bytes 49160 | tf_op jit(solution)/shard_map/ppermute | solution.py:27
  5.2 65.0 %collective-permute-start.1 = (f32[1,16,256]{2,1,0:T(8,128)S(1)}, f32[1,16,256]{2,1,0:T(8,128)S(1)}, u32[]{:S(2)}, u32[]{:S(2)}) collective-permute-start(f32[1,16,256]{2,1,0:T(8,128)S(1)} %get-tuple-element.80), channel_id=1, source_target_pairs={{32,0},{64,32},{96,64},{128,96},{160,128},{192,160},{224,192},{33,... | collective-permute-start | bytes 49160 | tf_op jit(solution)/shard_map/ppermute | solution.py:28
  55.6 65.6 %collective-permute-start.8 = (f32[1,8,128]{2,1,0:T(8,128)}, f32[1,8,128]{2,1,0:T(8,128)}, u32[]{:S(2)}, u32[]{:S(2)}) collective-permute-start(f32[1,8,128]{2,1,0:T(8,128)} %get-tuple-element.104), channel_id=1, source_target_pairs={{0,32},{32,64},{64,96},{96,128},{128,160},{160,192},{192,224},{1,3... | collective-permute-start | bytes 12296 | tf_op jit(solution)/shard_map/ppermute | solution.py:27
  59.3 64.1 %collective-permute-start.9 = (f32[1,8,128]{2,1,0:T(8,128)}, f32[1,8,128]{2,1,0:T(8,128)}, u32[]{:S(2)}, u32[]{:S(2)}) collective-permute-start(f32[1,8,128]{2,1,0:T(8,128)} %get-tuple-element.105), channel_id=1, source_target_pairs={{32,0},{64,32},{96,64},{128,96},{160,128},{192,160},{224,192},{33,... | collective-permute-start | bytes 12296 | tf_op jit(solution)/shard_map/ppermute | solution.py:28
  84.8 11.2 %collective-permute-start.4 = (f32[1,16,256]{2,1,0:T(8,128)S(1)}, f32[1,16,256]{2,1,0:T(8,128)S(1)}, u32[]{:S(2)}, u32[]{:S(2)}) collective-permute-start(f32[1,16,256]{2,1,0:T(8,128)S(1)} %get-tuple-element.76), channel_id=1, source_target_pairs={{0,32},{32,64},{64,96},{96,128},{128,160},{160,192},{192,224},{1,3... | collective-permute-start | bytes 49160 | tf_op jit(solution)/shard_map/ppermute | solution.py:27
  92.4 132.4 %collective-permute-start.20 = (f32[1,4,64]{2,1,0:T(4,128)}, f32[1,4,64]{2,1,0:T(4,128)}, u32[]{:S(2)}, u32[]{:S(2)}) collective-permute-start(f32[1,4,64]{2,1,0:T(4,128)} %get-tuple-element.126), channel_id=1, source_target_pairs={{0,32},{32,64},{64,96},{96,128},{128,160},{160,192},{192,224},{1,3... | collective-permute-start | bytes 3080 | tf_op jit(solution)/shard_map/ppermute | solution.py:27
  116.0 112.1 %collective-permute-start.21 = (f32[1,4,64]{2,1,0:T(4,128)}, f32[1,4,64]{2,1,0:T(4,128)}, u32[]{:S(2)}, u32[]{:S(2)}) collective-permute-start(f32[1,4,64]{2,1,0:T(4,128)} %get-tuple-element.127), channel_id=1, source_target_pairs={{32,0},{64,32},{96,64},{128,96},{160,128},{192,160},{224,192},{33,... | collective-permute-start | bytes 3080 | tf_op jit(solution)/shard_map/ppermute | solution.py:28
  118.1 12.6 %collective-permute-start.14 = (f32[34,1,256]{2,1,0:T(1,128)S(1)}, f32[34,1,256]{2,1,0:T(1,128)S(1)}, u32[]{:S(2)}, u32[]{:S(2)}) collective-permute-start(f32[34,1,256]{2,1,0:T(1,128)S(1)} %get-tuple-element.62), channel_id=1, source_target_pairs={{0,1},{1,2},{2,3},{3,4},{4,5},{5,6},{6,7},{7,8},{8,9},{9,10},{10,1... | collective-permute-start | bytes 104456 | tf_op jit(solution)/shard_map/ppermute | solution.py:27
  121.2 11.3 %collective-permute-start.15 = (f32[34,1,256]{2,1,0:T(1,128)S(1)}, f32[34,1,256]{2,1,0:T(1,128)S(1)}, u32[]{:S(2)}, u32[]{:S(2)}) collective-permute-start(f32[34,1,256]{2,1,0:T(1,128)S(1)} %get-tuple-element.63), channel_id=1, source_target_pairs={{1,0},{2,1},{3,2},{4,3},{5,4},{6,5},{7,6},{8,7},{9,8},{10,9},{11,1... | collective-permute-start | bytes 104456 | tf_op jit(solution)/shard_map/ppermute | solution.py:28
  124.2 57.8 %collective-permute-start.10 = (f32[18,1,128]{2,1,0:T(1,128)S(1)}, f32[18,1,128]{2,1,0:T(1,128)}, u32[]{:S(2)}, u32[]{:S(2)}) collective-permute-start(f32[18,1,128]{2,1,0:T(1,128)S(1)} %get-tuple-element.93), channel_id=1, source_target_pairs={{0,1},{1,2},{2,3},{3,4},{4,5},{5,6},{6,7},{7,8},{8,9},{9,10},{10,1... | collective-permute-start | bytes 27656 | tf_op jit(solution)/shard_map/ppermute | solution.py:27
  130.7 51.3 %collective-permute-start.11 = (f32[18,1,128]{2,1,0:T(1,128)S(1)}, f32[18,1,128]{2,1,0:T(1,128)S(1)}, u32[]{:S(2)}, u32[]{:S(2)}) collective-permute-start(f32[18,1,128]{2,1,0:T(1,128)S(1)} %get-tuple-element.92), channel_id=1, source_target_pairs={{1,0},{2,1},{3,2},{4,3},{5,4},{6,5},{7,6},{8,7},{9,8},{10,9},{11,1... | collective-permute-start | bytes 27656 | tf_op jit(solution)/shard_map/ppermute | solution.py:28
  183.7 11.4 %collective-permute-start.16 = (f32[1,8,128]{2,1,0:T(8,128)S(1)}, f32[1,8,128]{2,1,0:T(8,128)S(1)}, u32[]{:S(2)}, u32[]{:S(2)}) collective-permute-start(f32[1,8,128]{2,1,0:T(8,128)S(1)} %get-tuple-element.100), channel_id=1, source_target_pairs={{0,32},{32,64},{64,96},{96,128},{128,160},{160,192},{192,224},{1,3... | collective-permute-start | bytes 12296 | tf_op jit(solution)/shard_map/ppermute | solution.py:27
  191.5 144.2 %collective-permute-start.32 = (f32[1,2,32]{2,0,1:T(1,128)}, f32[1,2,32]{2,0,1:T(1,128)}, u32[]{:S(2)}, u32[]{:S(2)}) collective-permute-start(f32[1,2,32]{2,0,1:T(1,128)} %get-tuple-element.150), channel_id=1, source_target_pairs={{0,32},{32,64},{64,96},{96,128},{128,160},{160,192},{192,224},{1,3... | collective-permute-start | bytes 776 | tf_op jit(solution)/shard_map/ppermute | solution.py:27
  220.1 115.6 %collective-permute-start.33 = (f32[1,2,32]{2,0,1:T(1,128)}, f32[1,2,32]{2,0,1:T(1,128)}, u32[]{:S(2)}, u32[]{:S(2)}) collective-permute-start(f32[1,2,32]{2,0,1:T(1,128)} %get-tuple-element.151), channel_id=1, source_target_pairs={{32,0},{64,32},{96,64},{128,96},{160,128},{192,160},{224,192},{33,... | collective-permute-start | bytes 776 | tf_op jit(solution)/shard_map/ppermute | solution.py:28
  222.8 12.0 %collective-permute-start.26 = (f32[18,1,128]{2,1,0:T(1,128)S(1)}, f32[18,1,128]{2,1,0:T(1,128)S(1)}, u32[]{:S(2)}, u32[]{:S(2)}) collective-permute-start(f32[18,1,128]{2,1,0:T(1,128)S(1)} %get-tuple-element.88), channel_id=1, source_target_pairs={{0,1},{1,2},{2,3},{3,4},{4,5},{5,6},{6,7},{7,8},{8,9},{9,10},{10,1... | collective-permute-start | bytes 27656 | tf_op jit(solution)/shard_map/ppermute | solution.py:27
  224.8 12.1 %collective-permute-start.27 = (f32[18,1,128]{2,1,0:T(1,128)S(1)}, f32[18,1,128]{2,1,0:T(1,128)S(1)}, u32[]{:S(2)}, u32[]{:S(2)}) collective-permute-start(f32[18,1,128]{2,1,0:T(1,128)S(1)} %get-tuple-element.89), channel_id=1, source_target_pairs={{1,0},{2,1},{3,2},{4,3},{5,4},{6,5},{7,6},{8,7},{9,8},{10,9},{11,1... | collective-permute-start | bytes 27656 | tf_op jit(solution)/shard_map/ppermute | solution.py:28
  229.5 18.5 %collective-permute-start.22 = (f32[10,1,64]{2,1,0:T(1,128)}, f32[10,1,64]{2,1,0:T(1,128)}, u32[]{:S(2)}, u32[]{:S(2)}) collective-permute-start(f32[10,1,64]{2,1,0:T(1,128)} %get-tuple-element.115), channel_id=1, source_target_pairs={{0,1},{1,2},{2,3},{3,4},{4,5},{5,6},{6,7},{7,8},{8,9},{9,10},{10,1... | collective-permute-start | bytes 7688 | tf_op jit(solution)/shard_map/ppermute | solution.py:27
  234.8 13.2 %collective-permute-start.23 = (f32[10,1,64]{2,1,0:T(1,128)}, f32[10,1,64]{2,1,0:T(1,128)}, u32[]{:S(2)}, u32[]{:S(2)}) collective-permute-start(f32[10,1,64]{2,1,0:T(1,128)} %get-tuple-element.114), channel_id=1, source_target_pairs={{1,0},{2,1},{3,2},{4,3},{5,4},{6,5},{7,6},{8,7},{9,8},{10,9},{11,1... | collective-permute-start | bytes 7688 | tf_op jit(solution)/shard_map/ppermute | solution.py:28
  258.6 68.7 %collective-permute-start.30 = (f32[10,1,64]{2,1,0:T(1,128)S(1)}, f32[10,1,64]{2,1,0:T(1,128)S(1)}, u32[]{:S(2)}, u32[]{:S(2)}) collective-permute-start(f32[10,1,64]{2,1,0:T(1,128)S(1)} %get-tuple-element.112), channel_id=1, source_target_pairs={{0,1},{1,2},{2,3},{3,4},{4,5},{5,6},{6,7},{7,8},{8,9},{9,10},{10,1... | collective-permute-start | bytes 7688 | tf_op jit(solution)/shard_map/ppermute | solution.py:27
  265.6 61.8 %collective-permute-start.31 = (f32[10,1,64]{2,1,0:T(1,128)S(1)}, f32[10,1,64]{2,1,0:T(1,128)S(1)}, u32[]{:S(2)}, u32[]{:S(2)}) collective-permute-start(f32[10,1,64]{2,1,0:T(1,128)S(1)} %get-tuple-element.113), channel_id=1, source_target_pairs={{1,0},{2,1},{3,2},{4,3},{5,4},{6,5},{7,6},{8,7},{9,8},{10,9},{11,1... | collective-permute-start | bytes 7688 | tf_op jit(solution)/shard_map/ppermute | solution.py:28
  337.8 13.8 %collective-permute-start.38 = (f32[10,1,64]{2,1,0:T(1,128)S(1)}, f32[10,1,64]{2,1,0:T(1,128)S(1)}, u32[]{:S(2)}, u32[]{:S(2)}) collective-permute-start(f32[10,1,64]{2,1,0:T(1,128)S(1)} %get-tuple-element.110), channel_id=1, source_target_pairs={{0,1},{1,2},{2,3},{3,4},{4,5},{5,6},{6,7},{7,8},{8,9},{9,10},{10,1... | collective-permute-start | bytes 7688 | tf_op jit(solution)/shard_map/ppermute | solution.py:27
  340.5 11.1 %collective-permute-start.39 = (f32[10,1,64]{2,1,0:T(1,128)S(1)}, f32[10,1,64]{2,1,0:T(1,128)S(1)}, u32[]{:S(2)}, u32[]{:S(2)}) collective-permute-start(f32[10,1,64]{2,1,0:T(1,128)S(1)} %get-tuple-element.111), channel_id=1, source_target_pairs={{1,0},{2,1},{3,2},{4,3},{5,4},{6,5},{7,6},{8,7},{9,8},{10,9},{11,1... | collective-permute-start | bytes 7688 | tf_op jit(solution)/shard_map/ppermute | solution.py:28
  343.7 13.3 %collective-permute-start.34 = (f32[6,1,32]{2,0,1:T(8,128)}, f32[6,1,32]{2,0,1:T(8,128)}, u32[]{:S(2)}, u32[]{:S(2)}) collective-permute-start(f32[6,1,32]{2,0,1:T(8,128)} %get-tuple-element.137), channel_id=1, source_target_pairs={{0,1},{1,2},{2,3},{3,4},{4,5},{5,6},{6,7},{7,8},{8,9},{9,10},{10,1... | collective-permute-start | bytes 2312 | tf_op jit(solution)/shard_map/ppermute | solution.py:27
  367.6 10.9 %collective-permute-start.42 = (f32[6,1,32]{2,0,1:T(8,128)S(1)}, f32[6,1,32]{2,0,1:T(8,128)S(1)}, u32[]{:S(2)}, u32[]{:S(2)}) collective-permute-start(f32[6,1,32]{2,0,1:T(8,128)S(1)} %get-tuple-element.134), channel_id=1, source_target_pairs={{0,1},{1,2},{2,3},{3,4},{4,5},{5,6},{6,7},{7,8},{8,9},{9,10},{10,1... | collective-permute-start | bytes 2312 | tf_op jit(solution)/shard_map/ppermute | solution.py:27
  (93 other events, 2471.2 us)
where the time goes:
time: 707 us; the launch traced here: 702 us
  starting transfers between devices  249 us (35%)
  local copies, waits for them, and re-layouts  146 us (21%)
  blocking collectives  117 us (17%)
  waiting for transfers between devices  98.8 us (14%)
  other arithmetic  88.2 us (12%)
    ppermute x42, starting transfers between devices, with_halo(): before = lax.ppermute(last, axis, up)  152 us
    ppermute x42, waiting for transfers between devices, with_halo(): after = lax.ppermute(leading, axis, down)  98.7 us
    ppermute x42, starting transfers between devices, with_halo(): after = lax.ppermute(leading, axis, down)  97.6 us
    reshape x4, local copies, waits for them, and re-layouts, restrict(): field.reshape(size_x // 2, 2, size_y // 2, 2, size_z // 2, 2)  79.5 us
    all_gather x1, blocking collectives, collect(): lax.all_gather(conduct, ('gx', 'gy'), axis=0, tiled=True)  59.7 us
    all_gather x1, blocking collectives, collect(): lax.all_gather(source, ('gx', 'gy'), axis=0, tiled=True)  57.4 us
    reduce_sum x10, other arithmetic, restrict(): jnp.mean(field.reshape(size_x // 2, 2, size_y // 2, 2, size_z // 2, 2), a...  38.5 us
    reshape x3, local copies, waits for them, and re-layouts, prolong(): return grown.reshape(2 * size_x, 2 * size_y, 2 * size_z)  29.9 us
  transfers between devices with their start and end apart: 84, of which 28 were waited for; matrix products, arithmetic and copies ran while one was open for 22% of the time, Pallas kernels for 0%

commit v1 on v0

v1 whole, which is shorter than its diff:
```python
import functools

import jax
import jax.numpy as jnp
from jax import lax
from jax.experimental import pallas as pl
from jax.experimental.pallas import tpu as pltpu
from jax.sharding import PartitionSpec as P

MESH = pl.DeviceIdType.MESH
F32 = jnp.float32

SMOOTH_LO, SMOOTH_HI = 0.5, 2.0
COARSE_LO, COARSE_HI = 0.05, 2.0
BOTTOM = 8

STEPS = ((0, 1), (0, -1), (1, 0), (-1, 0), (1, 1), (1, -1), (-1, 1), (-1, -1))


def coefficients(low, high, sweeps):
    theta = (high + low) / 2.0
    delta = (high - low) / 2.0
    sigma = theta / delta
    rho = 1.0 / sigma
    pairs = []
    for _ in range(sweeps - 1):
        rho_next = 1.0 / (2.0 * sigma - rho)
        pairs.append((rho_next * rho, 2.0 * rho_next / delta))
        rho = rho_next
    return theta, pairs


THETA, ((MOMENTUM, STEP),) = coefficients(SMOOTH_LO, SMOOTH_HI, 2)


def harmonic(own, other):
    return 2.0 * own * other / (own + other)


def roll(value, shift, axis):
    size = value.shape[axis]
    return pltpu.roll(value, shift % size, axis)


def iota(shape, dim):
    return lax.broadcasted_iota(jnp.int32, shape, dim)


def times(rows, matrix):
    return jnp.dot(rows, matrix, precision=lax.Precision.HIGHEST, preferred_element_type=F32)


def loop(start, stop, body):
    def step(index, carry):
        body(index)
        return carry

    lax.fori_loop(start, stop, step, 0)


class Exchange:
    def __init__(self, field, left, right, send, recv, halo, depth):
        self.field, self.left, self.right = field, left, right
        self.send, self.recv = send, recv
        self.halo, self.depth = halo, depth
        self.planes = field.shape[0] - 2 * halo
        self.rows = field.shape[1] - 8

    def copies(self, place):
        h, n, r, x = self.halo, self.planes, self.depth, self.rows
        found = []
        for number, (dx, dy) in enumerate(STEPS):
            if dx == 0:
                source_plane = h + n - r if dy > 0 else h
                target_plane = h - r if dy > 0 else h + n
                source = self.field.at[pl.ds(source_plane, r), pl.ds(0, x)]
                target = self.field.at[pl.ds(target_plane, r), pl.ds(0, x)]
            else:
                count = n if dy == 0 else r - 1
                source_plane = h if dy <= 0 else h + n - count
                target_plane = h if dy == 0 else (h - count if dy > 0 else h + n)
                source = self.field.at[pl.ds(source_plane, count), pl.ds(x - 8 if dx > 0 else 0, 8)]
                landing = self.left if dx > 0 else self.right
                target = landing.at[pl.ds(target_plane, count)]
            found.append(
                pltpu.make_async_remote_copy(
                    src_ref=source,
                    dst_ref=target,
                    send_sem=self.send.at[number],
                    recv_sem=self.recv.at[number],
                    device_id=place(dx, dy),
                    device_id_type=MESH,
                )
            )
        return found

    def start(self, place):
        self.started = self.copies(place)
        for copy in self.started:
            copy.start()

    def arrive(self, which):
        for number in which:
            self.started[number].wait_recv()

    def merge(self, start, stop):
        x = self.rows
        shape = (8, self.field.shape[2])

        def body(p):
            upper = iota(shape, 0) < 4
            self.field[p, x:, :] = jnp.where(upper, self.right[p], self.left[p])

        loop(start, stop, body)

    def sent(self):
        for copy in self.started:
            copy.wait_send()


class Level:
    def __init__(self, number, lanes, refs, gx, gy, counts):
        self.scale = 0.25**number
        self.lanes = lanes
        self.gx, self.gy = gx, gy
        self.count_x, self.count_y = counts
        (self.k, self.b, self.xh, self.x1, self.x2, self.wx, self.wy, self.wz, self.w, self.inv, self.z0, self.z1) = refs
        self.h = self.k.halo
        self.n = self.k.planes
        self.x = self.k.rows
        self.shape = (self.x + 8, 128 * ((lanes + 127) // 128))
        self.period = lanes

    def row_ok(self):
        row = iota(self.shape, 0)
        below = jnp.where(self.gx == 0, 1, 0)
        above = jnp.where(self.gx == self.count_x - 1, 1, 0)
        bad_low = jnp.where(row >= self.x + 4, below, 0)
        bad_high = jnp.where((row >= self.x) & (row < self.x + 4), above, 0)
        return (bad_low + bad_high) == 0

    def plane_ok(self, p):
        y = self.gy * self.n + p - self.h
        return (y >= 0) & (y < self.count_y * self.n)

    def mend(self, start, stop):
        field, x = self.k.field, self.x
        tile = (8, self.shape[1])

        @pl.when(self.gx == self.count_x - 1)
        def _():
            def body(p):
                own = roll(field[p, x - 8 : x, :], 1, 0)
                field[p, x:, :] = jnp.where(iota(tile, 0) == 0, own, field[p, x:, :])

            loop(start, stop, body)

        @pl.when(self.gx == 0)
        def _():
            def body(p):
                own = roll(field[p, 0:8, :], 7, 0)
                field[p, x:, :] = jnp.where(iota(tile, 0) == 7, own, field[p, x:, :])

            loop(start, stop, body)

    def mend_planes(self):
        field, h, n = self.k.field, self.h, self.n

        @pl.when(self.gy == 0)
        def _():
            field[h - 1] = field[h]

        @pl.when(self.gy == self.count_y - 1)
        def _():
            field[h + n] = field[h + n - 1]

    def lane(self):
        return iota(self.shape, 1) % self.period

    def faces(self, start, stop):
        k = self.k.field

        def body(p):
            own = k[p]
            self.wx[p] = harmonic(own, roll(own, -1, 0))
            along = harmonic(own, roll(own, -1, 1))
            self.wz[p] = jnp.where(self.lane() == self.period - 1, 0.0, along)

        loop(start, stop, body)

    def faces_y(self, start, stop):
        k = self.k.field

        def body(p):
            self.wy[p] = harmonic(k[p], k[p + 1])

        loop(start, stop, body)

    def totals(self, start, stop):
        k = self.k.field

        def body(p):
            wx, wz = self.wx[p], self.wz[p]
            lane = self.lane()
            edge = jnp.where((lane == 0) | (lane == self.period - 1), k[p], 0.0)
            total = wx + roll(wx, 1, 0) + self.wy[p] + self.wy[p - 1] + wz + roll(wz, 1, 1) + edge
            self.w[p] = total
            ok = self.row_ok() & self.plane_ok(p)
            self.inv[p] = jnp.where(ok, 1.0 / total, 0.0)

        loop(start, stop, body)

    def beside(self, field, p):
        own, wx, wz = field[p], self.wx[p], self.wz[p]
        found = wx * roll(own, -1, 0) + roll(wx * own, 1, 0)
        found = found + self.wy[p] * field[p + 1] + self.wy[p - 1] * field[p - 1]
        return found + wz * roll(own, -1, 1) + roll(wz * own, 1, 1)

    def first(self, start, stop):
        b = self.b.field

        def body(p):
            self.x1[p] = b[p] * self.inv[p] * (1.0 / (THETA * self.scale))

        loop(start, stop, body)

    def second(self):
        h, n, x = self.h, self.n, self.x

        def body(p):
            own = self.x1[p]
            factor = 1.0 + MOMENTUM + STEP * (THETA - 1.0)
            self.x2[p] = factor * own + STEP * (self.inv[p] * self.beside(self.x1, p))

        loop(h - 1, h + n + 1, body)

        def keep(p):
            self.xh.field[p, 0:x, :] = self.x2[p, 0:x, :]

        loop(h, h + n, keep)

    def residual(self, field, p):
        return self.b.field[p] - self.scale * (self.w[p] * field[p] - self.beside(field, p))

    def correct(self, p, grown):
        ok = self.row_ok() & self.plane_ok(p)
        self.z0[p] = jnp.where(ok, self.xh.field[p] + grown, 0.0)

    def third(self, start, stop):
        def body(p):
            own = self.z0[p]
            flow = self.inv[p] * self.beside(self.z0, p)
            self.z1[p] = (1.0 - 1.0 / THETA) * own + self.x1[p] + (1.0 / THETA) * flow

        loop(start, stop, body)

    def fourth(self, start, stop, target):
        def body(p):
            own = self.z1[p]
            flow = self.inv[p] * self.beside(self.z1, p)
            found = (1.0 + MOMENTUM - STEP) * own - MOMENTUM * self.z0[p]
            target[p] = found + (STEP * THETA) * self.x1[p] + STEP * flow

        loop(start, stop, body)


class Whole:
    def __init__(self, number, size_z, per_block, refs):
        self.scale = 0.25**number
        self.size_z, self.per_block = size_z, per_block
        self.k, self.b, self.x1, self.x2, self.wx, self.wy, self.wz, self.w, self.inv, self.z0, self.z1 = refs
        self.count = self.k.shape[0] - 2
        self.shape = self.k.shape[1:]
        self.period = size_z * per_block

    def lane(self):
        return iota(self.shape, 1) % self.period

    def blank(self):
        for ref in (self.k, self.x1, self.x2, self.wx, self.z0, self.z1):
            ref[0] = jnp.zeros(self.shape, F32)
            ref[self.count + 1] = jnp.zeros(self.shape, F32)

    def after(self, ref, g):
        inner = self.lane() < self.period - self.size_z
        return jnp.where(inner, roll(ref[g], -self.size_z, 1), roll(ref[g + 1], -self.size_z, 1))

    def before(self, own, previous):
        inner = self.lane() >= self.size_z
        return jnp.where(inner, roll(own, self.size_z, 1), roll(previous, self.size_z, 1))

    def weights(self):
        rows = self.shape[0]

        def faces(g):
            own = self.k[g]
            lane, row = self.lane(), iota(self.shape, 0)
            end = jnp.where(lane >= self.period - self.size_z, jnp.where(g == self.count, 1, 0), 0)
            self.wx[g] = jnp.where(end == 1, 0.0, harmonic(own, self.after(self.k, g)))
            self.wy[g] = jnp.where(row == rows - 1, 0.0, harmonic(own, roll(own, -1, 0)))
            self.wz[g] = jnp.where(lane % self.size_z == self.size_z - 1, 0.0, harmonic(own, roll(own, -1, 1)))

        loop(1, self.count + 1, faces)

        def totals(g):
            lane, row = self.lane(), iota(self.shape, 0)
            high = jnp.where(lane >= self.period - self.size_z, jnp.where(g == self.count, 1.0, 0.0), 0.0)
            low = jnp.where(lane < self.size_z, jnp.where(g == 1, 1.0, 0.0), 0.0)
            edge = high + low
            edge = edge + jnp.where((row == 0) | (row == rows - 1), 1.0, 0.0)
            z = lane % self.size_z
            edge = edge + jnp.where((z == 0) | (z == self.size_z - 1), 1.0, 0.0)
            wx, wy, wz = self.wx[g], self.wy[g], self.wz[g]
            total = wx + self.before(wx, self.wx[g - 1]) + wy + roll(wy, 1, 0) + wz + roll(wz, 1, 1)
            total = total + edge * self.k[g]
            self.w[g] = total
            self.inv[g] = 1.0 / total

        loop(1, self.count + 1, totals)

    def beside(self, field, g):
        own, wx, wy, wz = field[g], self.wx[g], self.wy[g], self.wz[g]
        found = wx * self.after(field, g) + self.before(wx * own, self.wx[g - 1] * field[g - 1])
        found = found + wy * roll(own, -1, 0) + roll(wy * own, 1, 0)
        return found + wz * roll(own, -1, 1) + roll(wz * own, 1, 1)

    def down(self):
        def first(g):
            self.x1[g] = self.b[g] * self.inv[g] * (1.0 / (THETA * self.scale))

        loop(1, self.count + 1, first)

        def second(g):
            factor = 1.0 + MOMENTUM + STEP * (THETA - 1.0)
            self.x2[g] = factor * self.x1[g] + STEP * (self.inv[g] * self.beside(self.x1, g))

        loop(1, self.count + 1, second)

    def residual(self, g):
        return self.b[g] - self.scale * (self.w[g] * self.x2[g] - self.beside(self.x2, g))

    def up(self, target):
        def third(g):
            own = self.z0[g]
            flow = self.inv[g] * self.beside(self.z0, g)
            self.z1[g] = (1.0 - 1.0 / THETA) * own + self.x1[g] + (1.0 / THETA) * flow

        loop(1, self.count + 1, third)

        def fourth(g):
            flow = self.inv[g] * self.beside(self.z1, g)
            found = (1.0 + MOMENTUM - STEP) * self.z1[g] - MOMENTUM * self.z0[g]
            target(g, found + (STEP * THETA) * self.x1[g] + STEP * flow)

        loop(1, self.count + 1, fourth)

    def bottom(self):
        theta, pairs = coefficients(COARSE_LO, COARSE_HI, BOTTOM)

        def first(g):
            scaled = self.b[g] * self.inv[g] * (1.0 / self.scale)
            self.x2[g] = scaled
            self.x1[g] = scaled * (1.0 / theta)
            self.z0[g] = scaled * (1.0 / theta)

        loop(1, self.count + 1, first)
        now, later = self.z0, self.z1
        for momentum, step in pairs:

            def sweep(g, now=now, later=later, momentum=momentum, step=step):
                own = now[g]
                flow = self.inv[g] * self.beside(now, g)
                update = momentum * self.x1[g] + step * (self.x2[g] - own + flow)
                self.x1[g] = update
                later[g] = own + update

            loop(1, self.count + 1, sweep)
            now, later = later, now
        return now


def shrink_lanes(lanes, kept):
    row, col = iota((lanes, 128), 0), iota((lanes, 128), 1)
    return jnp.where(row // 2 == col % kept, 0.125, 0.0).astype(F32)


def grow_lanes(kept, lanes):
    row, col = iota((128, lanes), 0), iota((128, lanes), 1)
    period = 2 * kept
    return jnp.where((col % period) // 2 == row, 1.0, 0.0).astype(F32)


def halve_rows(pair, scratch, rows):
    parts = []
    for part in range(pair.shape[1] // 128):
        scratch[part, 0:rows, :] = pair[:, part * 128 : (part + 1) * 128]
    for part in range(pair.shape[1] // 128):
        even = scratch[part, pl.ds(0, rows // 2, stride=2), :]
        odd = scratch[part, pl.ds(1, rows // 2, stride=2), :]
        parts.append(even + odd)
    return parts[0] if len(parts) == 1 else jnp.concatenate(parts, axis=1)


def restrict(read, target, fine_plane, coarse_plane, rows, lanes, kept, scratch):
    matrix = shrink_lanes(128 * ((lanes + 127) // 128), kept)
    if lanes < 128:
        matrix = jnp.where(iota(matrix.shape, 0) < lanes, matrix, 0.0)
    target_rows = rows // 2

    def body(j):
        pair = read(fine_plane + 2 * j) + read(fine_plane + 2 * j + 1)
        target[coarse_plane + j, 0:target_rows, :] = times(halve_rows(pair, scratch, rows), matrix)

    return body


def double_rows(value, scratch, rows):
    own = 2 * (rows - 8)
    parts = []
    for part in range(value.shape[1] // 128):
        piece = value[:, part * 128 : (part + 1) * 128]
        scratch[part, pl.ds(0, rows, stride=2), :] = piece
        scratch[part, pl.ds(1, rows, stride=2), :] = piece
    for part in range(value.shape[1] // 128):
        upper = iota((8, 128), 0) < 4
        low, high = scratch[part, own : own + 8, :], scratch[part, own + 8 : own + 16, :]
        tail = jnp.where(upper, low, high)
        parts.append(jnp.concatenate([scratch[part, 0:own, :], tail], axis=0))
    return parts[0] if len(parts) == 1 else jnp.concatenate(parts, axis=1)


def kernel(count_x, count_y, names, *refs):
    r = dict(zip(names, refs))
    gx, gy = lax.axis_index("gx"), lax.axis_index("gy")
    ring_x = 4
    ring_z = count_y // ring_x
    chip_x, chip_z = gy % ring_x, gy // ring_x

    def place(dx, dy):
        return ((gx + dx + count_x) % count_x, (gy + dy + count_y) % count_y)

    def along_x(d):
        return (gx, chip_z * ring_x + (chip_x + d) % ring_x)

    def along_z(d):
        return (gx, ((chip_z + d) % ring_z) * ring_x + chip_x)

    def along_gx(d):
        return ((gx + d) % count_x, gy)

    partners = [place(dx, dy) for dx, dy in STEPS]
    partners += [along_x(d) for d in range(1, ring_x)]
    partners += [along_z(d) for d in range(1, ring_z)]
    partners += [along_gx(d) for d in range(1, count_x)]

    load_k = pltpu.make_async_copy(r["coefficient"], r["k_in"], r["load"].at[0])
    load_b = pltpu.make_async_copy(r["right_side"], r["b_in"], r["load"].at[1])
    load_k.start()
    load_b.start()
    barrier = pltpu.get_barrier_semaphore()
    for partner in partners:
        pl.semaphore_signal(barrier, inc=1, device_id=partner, device_id_type=MESH)

    def exchange(name, number, halo, depth):
        tag = f"{name}{number}"
        return Exchange(r[tag], r[tag + "_l"], r[tag + "_r"], r[tag + "_send"], r[tag + "_recv"], halo, depth)

    levels = []
    for number, (lanes, halo, depth_k, depth_b, depth_x) in enumerate(SHAPES):
        fields = [
            exchange("k", number, halo, depth_k),
            exchange("b", number, halo, depth_b),
            exchange("xh", number, halo, depth_x),
        ]
        fields += [r[f"{name}{number}"] for name in LOCAL]
        levels.append(Level(number, lanes, fields, gx, gy, (count_x, count_y)))
    l0, l1, l2 = levels
    l3 = Whole(3, 32, 4, [r[f"{name}3"] for name in WHOLE])
    l4 = Whole(4, 16, 2, [r[f"{name}4"] for name in WHOLE])

    def turn(staged, target):
        for y in range(l0.n):
            for part in range(2):
                lanes = pl.ds(128 * part, 128)
                target[l0.h + y, 0 : l0.x, lanes] = staged[part, pl.ds(y, l0.x, stride=l0.n), :]

    load_k.wait()
    turn(r["k_in"], r["k0"])
    load_b.wait()
    turn(r["b_in"], r["b0"])
    pl.semaphore_wait(barrier, len(partners))
    l0.k.start(place)
    l0.b.start(place)

    half = r["half"]
    k0, k1, k2 = r["k0"], r["k1"], r["k2"]
    loop(0, l1.n, restrict(lambda p: k0[p, 0 : l0.x, :], k1, l0.h, l1.h, l0.x, 256, 128, half))
    l1.k.start(place)
    loop(0, l2.n, restrict(lambda p: k1[p, 0 : l1.x, :], k2, l1.h, l2.h, l1.x, 128, 64, half))
    l2.k.start(place)

    def small_block(read):
        row, col = iota((128, 128), 0), iota((128, 128), 1)
        matrix = jnp.where((row < 64) & (row // 2 == col % 32), 0.125, 0.0).astype(F32)
        tile = (8, 128)
        mine = iota(tile, 1) // 32 == iota(tile, 0) // 2
        found = jnp.zeros(tile, F32)
        for j in range(2):
            pair = read(l2.h + 2 * j) + read(l2.h + 2 * j + 1)
            spread = jnp.where(mine, times(pair, matrix), 0.0)
            line = jnp.sum(spread, axis=0, keepdims=True)
            found = jnp.where(iota(tile, 0) == 2 * chip_x + j, jnp.broadcast_to(line, tile), found)
        return found

    class Gather:
        def __init__(self, name, target):
            self.first, self.target = r[name + "_first"], target
            self.send, self.recv = r[name + "_send"], r[name + "_recv"]
            self.all = []

        def go(self, base, source, target, where, count):
            copies = []
            for d in range(1, count):
                copies.append(
                    pltpu.make_async_remote_copy(
                        src_ref=source,
                        dst_ref=target,
                        send_sem=self.send.at[base + d - 1],
                        recv_sem=self.recv.at[base + d - 1],
                        device_id=where(d),
                        device_id_type=MESH,
                    )
                )
            for copy in copies:
                copy.start()
            self.now = copies
            self.all += copies

        def along_x(self, tile):
            self.first[chip_x] = tile
            slot = self.first.at[chip_x]
            self.go(0, slot, slot, along_x, ring_x)

        def along_z(self):
            self.arrive()
            rows = pl.ds(pl.multiple_of(8 * chip_z, 8), 8)
            found = self.first[0]
            for slot in range(1, ring_x):
                found = found + self.first[slot]
            self.target[gx + 1, rows, :] = found
            part = self.target.at[gx + 1, rows]
            self.go(ring_x - 1, part, part, along_z, ring_z)

        def along_gx(self):
            self.arrive()
            part = self.target.at[gx + 1]
            self.go(ring_x + ring_z - 2, part, part, along_gx, count_x)

        def arrive(self):
            for copy in self.now:
                copy.wait_recv()

    l3.blank()
    l4.blank()
    gather_k, gather_b = Gather("gk", l3.k), Gather("gb", l3.b)
    gather_k.along_x(small_block(lambda p: k2[p, 0 : l2.x, :]))

    def ready(level):
        h, n, depth = level.h, level.n, level.k.depth
        level.k.arrive((2, 3))
        level.k.merge(h, h + n)
        level.mend(h, h + n)
        level.faces(h, h + n)
        level.faces_y(h, h + n - 1)
        level.totals(h + 1, h + n - 1)
        level.k.arrive((0, 1, 4, 5, 6, 7))
        low, high = h - depth + 1, h + n + depth - 1
        level.k.merge(low, h)
        level.k.merge(h + n, high)
        level.mend(low, h)
        level.mend(h + n, high)
        level.mend_planes()
        level.faces(low, h)
        level.faces(h + n, high)
        level.faces_y(h - depth, h)
        level.faces_y(h + n - 1, high)
        level.totals(low, h + 1)
        level.totals(h + n - 1, high)

    def descend(level):
        h, n, depth = level.h, level.n, level.b.depth
        level.b.arrive(range(8))
        level.b.merge(h - depth + 1, h + n + depth - 1)
        level.first(h - depth, h + n + depth)
        level.second()

    ready(l0)
    descend(l0)
    loop(
        0,
        l1.n,
        restrict(lambda p: l0.residual(l0.x2, p)[0 : l0.x, :], r["b1"], l0.h, l1.h, l0.x, 256, 128, half),
    )
    l1.b.start(place)
    l0.xh.start(place)
    gather_k.along_z()
    ready(l1)
    descend(l1)
    loop(
        0,
        l2.n,
        restrict(lambda p: l1.residual(l1.x2, p)[0 : l1.x, :], r["b2"], l1.h, l2.h, l1.x, 128, 64, half),
    )
    l2.b.start(place)
    l1.xh.start(place)
    gather_k.along_gx()
    ready(l2)
    descend(l2)
    gather_b.along_x(small_block(lambda p: l2.residual(l2.x2, p)[0 : l2.x, :]))
    l2.xh.start(place)

    def to_bottom(read, target):
        row, col = iota((128, 128), 0), iota((128, 128), 1)
        same_x = (row // 32) // 2 == (col % 32) // 16
        same_z = (row % 32) // 2 == col % 16
        matrix = jnp.where(same_x & same_z, 0.125, 0.0).astype(F32)

        def body(g):
            target[g] = times(halve_rows(read(g), half, 64), matrix)

        loop(1, count_x + 1, body)

    gather_k.arrive()
    l3.weights()
    to_bottom(lambda g: l3.k[g], l4.k)
    l4.weights()
    gather_b.along_z()
    gather_b.along_gx()
    gather_b.arrive()
    l3.down()
    to_bottom(l3.residual, l4.b)
    deepest = l4.bottom()

    row, col = iota((128, 128), 0), iota((128, 128), 1)
    same = ((col // 32) // 2 == (row % 32) // 16) & ((col % 32) // 2 == row % 16) & (row < 32)
    matrix_43 = jnp.where(same, 1.0, 0.0).astype(F32)

    def lift(g):
        grown = times(deepest[g], matrix_43)
        half[0, pl.ds(0, 32, stride=2), :] = grown
        half[0, pl.ds(1, 32, stride=2), :] = grown
        l3.z0[g] = l3.x2[g] + half[0, 0:64, :]

    loop(1, count_x + 1, lift)
    answer = r["answer"]

    def store(g, value):
        answer[g - 1, 8:72, :] = value

    l3.up(store)

    matrix_32 = jnp.where(iota((128, 128), 0) % 32 == (iota((128, 128), 1) % 64) // 2, 1.0, 0.0).astype(F32)
    lower = jnp.maximum(gx - 1, 0)
    upper = jnp.minimum(gx + 1, count_x - 1)
    l2.xh.arrive(range(8))
    l2.xh.merge(l2.h - 3, l2.h + l2.n + 3)
    tile = (8, 128)
    group = iota(tile, 1) // 32 == iota(tile, 0) // 2
    first_half = iota(tile, 0) < 4

    def lift_2(j):
        at = 6 + 2 * gy + j
        own = jnp.broadcast_to(answer[gx, pl.ds(at, 1), :], tile)
        high = jnp.broadcast_to(answer[upper, pl.ds(at, 1), :], tile)
        low = jnp.broadcast_to(answer[lower, pl.ds(at, 1), :], tile)
        halo = jnp.where(first_half, high, low)
        spread = jnp.concatenate([jnp.where(group, own, 0.0), jnp.where(group, halo, 0.0)], axis=0)
        grown = times(spread, matrix_32)
        l2.correct(2 * j, grown)
        l2.correct(2 * j + 1, grown)

    loop(0, 6, lift_2)
    l2.third(1, 11)
    l2.fourth(2, 10, r["z2"])

    matrix_21 = grow_lanes(64, 128)
    l1.xh.arrive(range(8))
    l1.xh.merge(l1.h - 3, l1.h + l1.n + 3)

    def lift_1(j):
        grown = double_rows(times(r["z2"][2 + j], matrix_21), half, 16)
        l1.correct(2 * j, grown)
        l1.correct(2 * j + 1, grown)

    loop(0, 8, lift_1)
    l1.third(1, 15)
    l1.fourth(2, 14, r["z1out"])

    matrix_10 = grow_lanes(128, 256)
    l0.xh.arrive(range(8))
    l0.xh.merge(l0.h - 2, l0.h + l0.n + 2)

    def lift_0(j):
        grown = double_rows(times(r["z1out"][2 + j], matrix_10), half, 24)

        @pl.when(j > 0)
        def _():
            l0.correct(2 * j - 1, grown)

        @pl.when(j < 11)
        def _():
            l0.correct(2 * j, grown)

    loop(0, 12, lift_0)
    l0.third(1, 21)
    l0.fourth(2, 20, l0.x2)

    def finish(y):
        p = l0.h + y
        left = l0.residual(l0.x2, p)
        for part in range(2):
            lanes = slice(128 * part, 128 * (part + 1))
            r["k_in"][part, pl.ds(y, l0.x, stride=l0.n), :] = l0.x2[p, 0 : l0.x, lanes]
            r["b_in"][part, pl.ds(y, l0.x, stride=l0.n), :] = left[0 : l0.x, lanes]

    for y in range(l0.n):
        finish(y)
    stores = []
    for number, (staged, target) in enumerate(((r["k_in"], r["solution"]), (r["b_in"], r["residual"]))):
        stores.append(pltpu.make_async_copy(staged, target, r["load"].at[2 + number]))
    for copy in stores:
        copy.start()
    for level in levels:
        for field in (level.k, level.b, level.xh):
            field.sent()
    for copy in gather_k.all + gather_b.all:
        copy.wait_send()
    for copy in stores:
        copy.wait()


SHAPES = ((256, 3, 3, 2, 3), (128, 4, 4, 3, 4), (64, 4, 4, 3, 4))
LOCAL = ("x1_", "x2_", "wx", "wy", "wz", "w", "inv", "z0_", "z1_")
WHOLE = ("k", "b", "x1_", "x2_", "wx", "wy", "wz", "w", "inv", "z0_", "z1_")


def per_device(count_x, count_y, right_side, coefficient):
    nx, ny, nz = right_side.shape
    vmem = lambda *shape: pltpu.VMEM(shape, F32)
    scratch = {
        "k_in": vmem(2, nx * ny, 128),
        "b_in": vmem(2, nx * ny, 128),
        "load": pltpu.SemaphoreType.DMA((4,)),
        "half": vmem(2, 64, 128),
    }
    for number, (lanes, halo, *_) in enumerate(SHAPES):
        rows, planes, width = nx >> number, ny >> number, max(128, lanes)
        full = (planes + 2 * halo, rows + 8, width)
        for name in ("k", "b", "xh"):
            tag = f"{name}{number}"
            scratch[tag] = vmem(*full)
            scratch[tag + "_l"] = vmem(full[0], 8, width)
            scratch[tag + "_r"] = vmem(full[0], 8, width)
            scratch[tag + "_send"] = pltpu.SemaphoreType.DMA((8,))
            scratch[tag + "_recv"] = pltpu.SemaphoreType.DMA((8,))
        for name in LOCAL:
            scratch[f"{name}{number}"] = vmem(*full)
    for number, rows in ((3, 2 * count_y), (4, count_y)):
        for name in WHOLE:
            scratch[f"{name}{number}"] = vmem(count_x + 2, rows, 128)
    for name in ("gk", "gb"):
        scratch[name + "_first"] = vmem(4, 8, 128)
        scratch[name + "_send"] = pltpu.SemaphoreType.DMA((3 + count_y // 4 - 1 + count_x - 1,))
        scratch[name + "_recv"] = pltpu.SemaphoreType.DMA((3 + count_y // 4 - 1 + count_x - 1,))
    scratch["answer"] = vmem(count_x, 2 * count_y + 16, 128)
    scratch["z2"] = vmem((ny >> 2) + 8, (nx >> 2) + 8, 128)
    scratch["z1out"] = vmem((ny >> 1) + 8, (nx >> 1) + 8, 128)

    split = lambda value: value.reshape(nx * ny, 2, 128).transpose(1, 0, 2)
    join = lambda value: value.transpose(1, 0, 2).reshape(nx, ny, nz)
    names = ["right_side", "coefficient", "solution", "residual"] + list(scratch)
    shape = jax.ShapeDtypeStruct((2, nx * ny, 128), F32)
    found = pl.pallas_call(
        functools.partial(kernel, count_x, count_y, names),
        out_shape=(shape, shape),
        in_specs=[pl.BlockSpec(memory_space=pl.ANY)] * 2,
        out_specs=(pl.BlockSpec(memory_space=pl.ANY),) * 2,
        scratch_shapes=list(scratch.values()),
        compiler_params=pltpu.CompilerParams(
            collective_id=0, has_side_effects=True, vmem_limit_bytes=56 << 20
        ),
        name="vcycle",
    )(split(right_side), split(coefficient))
    return tuple(join(value) for value in found)


def solution(mesh):
    spec = P("gx", "gy", None)
    step = functools.partial(per_device, mesh.shape["gx"], mesh.shape["gy"])
    return jax.shard_map(step, mesh=mesh, in_specs=(spec, spec), out_specs=(spec, spec), check_vma=False)
```

time: 707 us -> 86.9 us (0.12)
  the two profiles are of different devices: /device:TPU:103 before, /device:TPU:1 now
where the time goes in v1:
time: 86.9 us; the launch traced here: 86.7 us
  Pallas kernels  79.1 us (91%)
  local copies, waits for them, and re-layouts  6.95 us (8%)
    pallas_call x1, Pallas kernels, per_device(): pl.pallas_call(functools.partial(kernel, count_x, count_y, names), out_sh...  79.1 us
    reshape x2, local copies, waits for them, and re-layouts, per_device(): join = lambda value: value.transpose(1, 0, 2).reshape(nx, ny, nz)  2.43 us
    transpose x2, local copies, waits for them, and re-layouts, per_device(): join = lambda value: value.transpose(1, 0, 2).reshape(nx, ny, nz)  1.85 us

profile of v1, /device:TPU:1, one launch (start us, length us, event | category | flops | bytes accessed | tf_op | source)
XLA Modules:
  0.0 86.7 jit_solution(16774466751114214595)
XLA Ops:
  0.6 0.0 copy-start
  0.6 1.4 %reshape.16 = f32[512,2,128]{2,1,0:T(2,128)S(1)} reshape(f32[32,16,256]{2,1,0:T(8,128)} %param.2) | data formatting | bytes 1048576 | tf_op jit(solution)/shard_map/reshape | solution.py:779
  2.0 0.0 copy-done
  2.0 0.3 reshape.17
  2.3 1.0 %copy_bitcast_fusion = (f32[2,512,128]{2,1,0:T(8,128)}, f32[2,512,128]{2,1,0:T(8,128)}) fusion(f32[512,2,128]{2,1,0:T(2,128)S(1)} %reshape.17, f32[512,2,128]{2,1,0:T(2,128)S(1)} %reshape.16), kind=kLoop, calls=%fused_computation | loop fusion | bytes 2097152 | tf_op jit(solution)/shard_map/transpose | solution.py:779
  3.3 79.1 %vcycle.1 = (f32[2,512,128]{2,1,0:T(8,128)}, f32[2,512,128]{2,1,0:T(8,128)}) custom-call(f32[2,512,128]{2,1,0:T(8,128)} %get-tuple-element.7.refs_0_, f32[2,512,128]{2,1,0:T(8,128)} %get-tuple-element.6.refs_1_), custom_call_target="tpu_custom_call" | custom-call | tf_op jit(solution)/shard_map/vcycle/pallas_call | solution.py:783
  82.4 1.4 %copy.6 = f32[512,2,128]{2,1,0:T(2,128)S(1)} copy(f32[512,2,128]{2,0,1:T(8,128)} %bitcast.7) | data formatting | bytes 1048576 | tf_op jit(solution)/shard_map/transpose | solution.py:780
  83.9 0.0 copy-start.1
  83.9 1.2 %reshape.18 = f32[32,16,256]{2,1,0:T(8,128)} reshape(f32[512,2,128]{2,1,0:T(2,128)S(1)} %copy.6) | data formatting | bytes 1048576 | tf_op jit(solution)/shard_map/reshape | solution.py:780
  85.1 0.0 copy-done.1
  85.1 0.4 copy.7
  85.5 1.2 %reshape.19 = f32[32,16,256]{2,1,0:T(8,128)} reshape(f32[512,2,128]{2,1,0:T(2,128)S(1)} %copy.7) | data formatting | bytes 1048576 | tf_op jit(solution)/shard_map/reshape | solution.py:780
Async XLA Ops:
  0.6 1.4 %copy-start = (f32[32,16,256]{2,1,0:T(8,128)S(1)}, f32[32,16,256]{2,1,0:T(8,128)}, u32[]{:S(2)}) copy-start(f32[32,16,256]{2,1,0:T(8,128)} %param.3) | copy-start | bytes 1572868
  83.9 1.2 %copy-start.1 = (f32[2,512,128]{2,1,0:T(8,128)S(1)}, f32[2,512,128]{2,1,0:T(8,128)}, u32[]{:S(2)}) copy-start(f32[2,512,128]{2,1,0:T(8,128)} %get-tuple-element.5) | copy-start | bytes 1572868

commit v2 on v1

v2 whole, which is shorter than its diff:
```python
import functools

import jax
import jax.numpy as jnp
from jax import lax
from jax.experimental import pallas as pl
from jax.experimental.pallas import tpu as pltpu
from jax.sharding import PartitionSpec as P

MESH = pl.DeviceIdType.MESH
F32 = jnp.float32

SMOOTH_LO, SMOOTH_HI = 0.5, 2.0
COARSE_LO, COARSE_HI = 0.05, 2.0
BOTTOM = 8

STEPS = ((0, 1), (0, -1), (1, 0), (-1, 0), (1, 1), (1, -1), (-1, 1), (-1, -1))


def coefficients(low, high, sweeps):
    theta = (high + low) / 2.0
    delta = (high - low) / 2.0
    sigma = theta / delta
    rho = 1.0 / sigma
    pairs = []
    for _ in range(sweeps - 1):
        rho_next = 1.0 / (2.0 * sigma - rho)
        pairs.append((rho_next * rho, 2.0 * rho_next / delta))
        rho = rho_next
    return theta, pairs


THETA, ((MOMENTUM, STEP),) = coefficients(SMOOTH_LO, SMOOTH_HI, 2)


def harmonic(own, other):
    return 2.0 * own * other / (own + other)


def roll(value, shift, axis):
    size = value.shape[axis]
    return pltpu.roll(value, shift % size, axis)


def iota(shape, dim):
    return lax.broadcasted_iota(jnp.int32, shape, dim)


def times(rows, matrix):
    high = rows.astype(jnp.bfloat16)
    rest = rows - high.astype(F32)
    middle = rest.astype(jnp.bfloat16)
    low = (rest - middle.astype(F32)).astype(jnp.bfloat16)
    found = [jnp.dot(term, matrix, preferred_element_type=F32) for term in (low, middle, high)]
    return (found[0] + found[1]) + found[2]


def loop(start, stop, body, unroll=1):
    count = (stop - start) // unroll

    def step(index, carry):
        for k in range(unroll):
            body(start + index * unroll + k)
        return carry

    if count > 1:
        lax.fori_loop(0, count, step, 0)
        start += count * unroll
    for index in range(start, stop):
        body(index)


class Exchange:
    def __init__(self, field, left, right, send, recv, halo, depth):
        self.field, self.left, self.right = field, left, right
        self.send, self.recv = send, recv
        self.halo, self.depth = halo, depth
        self.planes = field.shape[0] - 2 * halo
        self.rows = field.shape[1] - 8

    def copies(self, place):
        h, n, r, x = self.halo, self.planes, self.depth, self.rows
        found = []
        for number, (dx, dy) in enumerate(STEPS):
            if dx == 0:
                source_plane = h + n - r if dy > 0 else h
                target_plane = h - r if dy > 0 else h + n
                source = self.field.at[pl.ds(source_plane, r), pl.ds(0, x)]
                target = self.field.at[pl.ds(target_plane, r), pl.ds(0, x)]
            else:
                count = n if dy == 0 else r - 1
                source_plane = h if dy <= 0 else h + n - count
                target_plane = h if dy == 0 else (h - count if dy > 0 else h + n)
                source = self.field.at[pl.ds(source_plane, count), pl.ds(x - 8 if dx > 0 else 0, 8)]
                landing = self.left if dx > 0 else self.right
                target = landing.at[pl.ds(target_plane, count)]
            found.append(
                pltpu.make_async_remote_copy(
                    src_ref=source,
                    dst_ref=target,
                    send_sem=self.send.at[number],
                    recv_sem=self.recv.at[number],
                    device_id=place(dx, dy),
                    device_id_type=MESH,
                )
            )
        return found

    def start(self, place):
        self.started = self.copies(place)
        for copy in self.started:
            copy.start()

    def arrive(self, which):
        for number in which:
            self.started[number].wait_recv()

    def merge(self, start, stop):
        x = self.rows
        shape = (8, self.field.shape[2])

        def body(p):
            upper = iota(shape, 0) < 4
            self.field[p, x:, :] = jnp.where(upper, self.right[p], self.left[p])

        loop(start, stop, body, 4)

    def merge_mended(self, start, stop, at_low, at_high):
        x = self.rows
        shape = (8, self.field.shape[2])
        row = iota(shape, 0)
        take_high = jnp.where(row == 0, at_high, 0) == 1
        take_low = jnp.where(row == 7, at_low, 0) == 1
        upper = row < 4

        def body(p):
            tile = jnp.where(upper, self.right[p], self.left[p])
            tile = jnp.where(take_high, roll(self.field[p, x - 8 : x, :], 1, 0), tile)
            self.field[p, x:, :] = jnp.where(take_low, roll(self.field[p, 0:8, :], 7, 0), tile)

        loop(start, stop, body, 4)

    def sent(self):
        for copy in self.started:
            copy.wait_send()


class Level:
    def __init__(self, number, lanes, refs, gx, gy, counts):
        self.scale = 0.25**number
        self.lanes = lanes
        self.gx, self.gy = gx, gy
        self.count_x, self.count_y = counts
        (self.k, self.b, self.xh, self.x1, self.x2, self.wx, self.wy, self.wz, self.w, self.inv, self.z0, self.z1) = refs
        self.h = self.k.halo
        self.n = self.k.planes
        self.x = self.k.rows
        self.shape = (self.x + 8, 128 * ((lanes + 127) // 128))
        self.period = lanes
        self.unroll = 2 if number == 0 else 4

    def merge_k(self, start, stop):
        at_low = jnp.where(self.gx == 0, 1, 0)
        at_high = jnp.where(self.gx == self.count_x - 1, 1, 0)
        self.k.merge_mended(start, stop, at_low, at_high)

    def row_ok(self):
        row = iota(self.shape, 0)
        below = jnp.where(self.gx == 0, 1, 0)
        above = jnp.where(self.gx == self.count_x - 1, 1, 0)
        bad_low = jnp.where(row >= self.x + 4, below, 0)
        bad_high = jnp.where((row >= self.x) & (row < self.x + 4), above, 0)
        return (bad_low + bad_high) == 0

    def plane_ok(self, p):
        y = self.gy * self.n + p - self.h
        return (y >= 0) & (y < self.count_y * self.n)

    def mend_planes(self):
        field, h, n = self.k.field, self.h, self.n

        @pl.when(self.gy == 0)
        def _():
            field[h - 1] = field[h]

        @pl.when(self.gy == self.count_y - 1)
        def _():
            field[h + n] = field[h + n - 1]

    def lane(self):
        return iota(self.shape, 1) % self.period

    def faces(self, start, stop):
        k = self.k.field

        def body(p):
            own = k[p]
            self.wx[p] = harmonic(own, roll(own, -1, 0))
            along = harmonic(own, roll(own, -1, 1))
            self.wz[p] = jnp.where(self.lane() == self.period - 1, 0.0, along)

        loop(start, stop, body, self.unroll)

    def faces_y(self, start, stop):
        k = self.k.field

        def body(p):
            self.wy[p] = harmonic(k[p], k[p + 1])

        loop(start, stop, body, self.unroll)

    def totals(self, start, stop):
        k = self.k.field
        rows_ok = self.row_ok()

        def body(p):
            wx, wz = self.wx[p], self.wz[p]
            lane = self.lane()
            edge = jnp.where((lane == 0) | (lane == self.period - 1), k[p], 0.0)
            total = wx + roll(wx, 1, 0) + self.wy[p] + self.wy[p - 1] + wz + roll(wz, 1, 1) + edge
            self.w[p] = total
            ok = rows_ok & self.plane_ok(p)
            self.inv[p] = jnp.where(ok, 1.0 / total, 0.0)

        loop(start, stop, body, self.unroll)

    def beside(self, field, p):
        own, wx, wz = field[p], self.wx[p], self.wz[p]
        found = wx * roll(own, -1, 0) + roll(wx * own, 1, 0)
        found = found + self.wy[p] * field[p + 1] + self.wy[p - 1] * field[p - 1]
        return found + wz * roll(own, -1, 1) + roll(wz * own, 1, 1)

    def first(self, start, stop):
        b = self.b.field

        def body(p):
            self.x1[p] = b[p] * self.inv[p] * (1.0 / (THETA * self.scale))

        loop(start, stop, body, self.unroll)

    def second(self):
        h, n, x = self.h, self.n, self.x

        def value(p):
            own = self.x1[p]
            factor = 1.0 + MOMENTUM + STEP * (THETA - 1.0)
            return factor * own + STEP * (self.inv[p] * self.beside(self.x1, p))

        def inner(p):
            found = value(p)
            self.x2[p] = found
            self.xh.field[p, 0:x, :] = found[0:x, :]

        loop(h, h + n, inner, self.unroll)
        for p in (h - 1, h + n):
            self.x2[p] = value(p)

    def residual(self, field, p):
        return self.b.field[p] - self.scale * (self.w[p] * field[p] - self.beside(field, p))

    def correct(self, p, grown):
        ok = self.rows_ok & self.plane_ok(p)
        self.z0[p] = jnp.where(ok, self.xh.field[p] + grown, 0.0)

    def third(self, start, stop):
        def body(p):
            own = self.z0[p]
            flow = self.inv[p] * self.beside(self.z0, p)
            self.z1[p] = (1.0 - 1.0 / THETA) * own + self.x1[p] + (1.0 / THETA) * flow

        loop(start, stop, body, self.unroll)

    def fourth(self, start, stop, target):
        def body(p):
            own = self.z1[p]
            flow = self.inv[p] * self.beside(self.z1, p)
            found = (1.0 + MOMENTUM - STEP) * own - MOMENTUM * self.z0[p]
            target[p] = found + (STEP * THETA) * self.x1[p] + STEP * flow

        loop(start, stop, body, self.unroll)


LOW, HIGH = 8, 16


class Whole:
    def __init__(self, refs):
        self.scale = 0.25**3
        self.size_z = 32
        self.k, self.b, self.x1, self.x2, self.wx, self.wy, self.wz, self.w, self.inv = refs
        self.count = self.k.shape[0] - 2
        self.rows = self.k.shape[1] - LOW - HIGH
        self.shape = (self.rows, 128)

    def blank(self):
        for ref in (self.k, self.x1, self.x2, self.wx, self.wy, self.wz, self.inv):
            empty = jnp.zeros(ref.shape[1:], F32)
            ref[0] = empty
            ref[self.count + 1] = empty

            def body(g, ref=ref):
                ref[g, 0:LOW, :] = jnp.zeros((LOW, 128), F32)
                ref[g, LOW + self.rows :, :] = jnp.zeros((HIGH, 128), F32)

            loop(1, self.count + 1, body, 4)

    def at(self, ref, g):
        return ref[g, LOW : LOW + self.rows, :]

    def after(self, own, following):
        inner = iota(own.shape, 1) < 128 - self.size_z
        return jnp.where(inner, roll(own, -self.size_z, 1), roll(following, -self.size_z, 1))

    def before(self, own, previous):
        inner = iota(own.shape, 1) >= self.size_z
        return jnp.where(inner, roll(own, self.size_z, 1), roll(previous, self.size_z, 1))

    def weights(self):
        rows, inside = self.rows, slice(LOW, LOW + self.rows)

        def faces(g):
            own, following = self.at(self.k, g), self.at(self.k, g + 1)
            lane, row = iota(self.shape, 1), iota(self.shape, 0)
            end = jnp.where(lane >= 128 - self.size_z, jnp.where(g == self.count, 1, 0), 0)
            self.wx[g, inside, :] = jnp.where(end == 1, 0.0, harmonic(own, self.after(own, following)))
            self.wy[g, inside, :] = jnp.where(row == rows - 1, 0.0, harmonic(own, roll(own, -1, 0)))
            last = lane % self.size_z == self.size_z - 1
            self.wz[g, inside, :] = jnp.where(last, 0.0, harmonic(own, roll(own, -1, 1)))

        loop(1, self.count + 1, faces)

        def totals(g):
            lane, row = iota(self.shape, 1), iota(self.shape, 0)
            high = jnp.where(lane >= 128 - self.size_z, jnp.where(g == self.count, 1.0, 0.0), 0.0)
            low = jnp.where(lane < self.size_z, jnp.where(g == 1, 1.0, 0.0), 0.0)
            edge = high + low
            edge = edge + jnp.where((row == 0) | (row == rows - 1), 1.0, 0.0)
            z = lane % self.size_z
            edge = edge + jnp.where((z == 0) | (z == self.size_z - 1), 1.0, 0.0)
            wx, wy, wz = self.at(self.wx, g), self.at(self.wy, g), self.at(self.wz, g)
            total = wx + self.before(wx, self.at(self.wx, g - 1)) + wy + roll(wy, 1, 0) + wz + roll(wz, 1, 1)
            total = total + edge * self.at(self.k, g)
            self.w[g, inside, :] = total
            self.inv[g, inside, :] = 1.0 / total

        loop(1, self.count + 1, totals)

    def flow(self, fields, weights):
        previous, own, following = fields
        wx_previous, wx, wy, wz = weights
        found = wx * self.after(own, following) + self.before(wx * own, wx_previous * previous)
        found = found + wy * roll(own, -1, 0) + roll(wy * own, 1, 0)
        return found + wz * roll(own, -1, 1) + roll(wz * own, 1, 1)

    def beside(self, field, g):
        fields = [self.at(field, g + step) for step in (-1, 0, 1)]
        weights = [self.at(self.wx, g - 1)] + [self.at(ref, g) for ref in (self.wx, self.wy, self.wz)]
        return self.flow(fields, weights)

    def down(self, left):
        inside = slice(LOW, LOW + self.rows)

        def first(g):
            found = self.at(self.b, g) * self.at(self.inv, g) * (1.0 / (THETA * self.scale))
            self.x1[g, inside, :] = found

        loop(1, self.count + 1, first, 2)

        def second(g):
            factor = 1.0 + MOMENTUM + STEP * (THETA - 1.0)
            moved = self.at(self.inv, g) * self.beside(self.x1, g)
            self.x2[g, inside, :] = factor * self.at(self.x1, g) + STEP * moved

        loop(1, self.count + 1, second, 2)

        def residual(g):
            applied = self.at(self.w, g) * self.at(self.x2, g) - self.beside(self.x2, g)
            left[g - 1] = self.at(self.b, g) - self.scale * applied

        loop(1, self.count + 1, residual, 2)

    def up(self, gx, start, grown, held, answer):
        span = pl.ds(start, 24)
        z0, z1 = held
        planes = (0, 1, 2)
        part = lambda ref, c: ref[gx + c, span, :]
        for c in planes:
            z0[c + 1] = part(self.x2, c) + grown[c, span, :]

        def flow(field, c):
            fields = [field[c + step] for step in (0, 1, 2)]
            before = self.wx[jnp.maximum(gx + c - 1, 0), span, :]
            return part(self.inv, c) * self.flow(fields, [before, part(self.wx, c), part(self.wy, c), part(self.wz, c)])

        for c in planes:
            z1[c + 1] = (1.0 - 1.0 / THETA) * z0[c + 1] + part(self.x1, c) + (1.0 / THETA) * flow(z0, c)
        for c in planes:
            found = (1.0 + MOMENTUM - STEP) * z1[c + 1] - MOMENTUM * z0[c + 1]
            answer[c] = found + (STEP * THETA) * part(self.x1, c) + STEP * flow(z1, c)


class Deepest:
    def __init__(self, count):
        self.count = count
        self.scale = 0.25**4
        shape = (8, 128)
        self.lane, self.row = iota(shape, 1), iota(shape, 0)
        self.low_x = (self.lane % 32) < 16
        self.zero = jnp.zeros(shape, F32)

    def next_x(self, tiles):
        back, ahead = [roll(t, -16, 1) for t in tiles], [roll(t, 16, 1) for t in tiles] + [self.zero]
        return [jnp.where(self.low_x, back[g], ahead[g + 1]) for g in range(self.count)]

    def last_x(self, tiles):
        back, ahead = [self.zero] + [roll(t, -16, 1) for t in tiles], [roll(t, 16, 1) for t in tiles]
        return [jnp.where(self.low_x, back[g], ahead[g]) for g in range(self.count)]

    def next_y(self, tiles):
        moved = [roll(t, -1, 0) for t in tiles]
        return [jnp.where(self.row < 7, t, roll(t, -32, 1)) for t in moved]

    def last_y(self, tiles):
        moved = [roll(t, 1, 0) for t in tiles]
        return [jnp.where(self.row > 0, t, roll(t, 32, 1)) for t in moved]

    def next_z(self, tiles):
        return [roll(t, -1, 1) for t in tiles]

    def last_z(self, tiles):
        return [roll(t, 1, 1) for t in tiles]

    def weights(self, k, weight_refs, inv_ref):
        lane, row, span = self.lane, self.row, range(self.count)
        z = lane % 16
        end_y = (row == 7) & (lane >= 96)
        edge = jnp.where((z == 0) | (z == 15), 1.0, 0.0)
        edge = edge + jnp.where(end_y | ((row == 0) & (lane < 32)), 1.0, 0.0)
        faces_x = [harmonic(a, b) for a, b in zip(k, self.next_x(k))]
        faces_x[-1] = jnp.where(self.low_x, faces_x[-1], 0.0)
        faces_y = [jnp.where(end_y, 0.0, harmonic(a, b)) for a, b in zip(k, self.next_y(k))]
        faces_z = [jnp.where(z == 15, 0.0, harmonic(a, b)) for a, b in zip(k, self.next_z(k))]
        sets = [faces_x, self.last_x(faces_x), faces_y, self.last_y(faces_y), faces_z, self.last_z(faces_z)]
        for g in span:
            total = edge * k[g]
            if g == 0:
                total = total + jnp.where(self.low_x, k[g], 0.0)
            if g == self.count - 1:
                total = total + jnp.where(self.low_x, 0.0, k[g])
            for one in sets:
                total = total + one[g]
            inv = 1.0 / total
            inv_ref[g] = inv
            for number, one in enumerate(sets):
                weight_refs[number, g] = one[g] * inv

    def solve(self, b, weight_refs, inv_ref):
        theta, pairs = coefficients(COARSE_LO, COARSE_HI, BOTTOM)
        span = range(self.count)
        scaled = [b[g] * inv_ref[g] * (1.0 / self.scale) for g in span]
        update = [t * (1.0 / theta) for t in scaled]
        found = update
        for momentum, step in pairs:
            shifted = [
                self.next_x(found),
                self.last_x(found),
                self.next_y(found),
                self.last_y(found),
                self.next_z(found),
                self.last_z(found),
            ]
            following = []
            for g in span:
                flow = weight_refs[0, g] * shifted[0][g]
                for number in range(1, 6):
                    flow = flow + weight_refs[number, g] * shifted[number][g]
                following.append(momentum * update[g] + step * ((scaled[g] - found[g]) + flow))
            update = following
            found = [a + d for a, d in zip(found, update)]
        return found


def shrink_lanes(lanes, kept):
    row, col = iota((max(lanes, 128), 128), 0), iota((max(lanes, 128), 128), 1)
    return jnp.where((row // 2 == col % kept) & (row < lanes), 0.125, 0.0).astype(jnp.bfloat16)


def grow_lanes(kept, lanes):
    row, col = iota((128, lanes), 0), iota((128, lanes), 1)
    period = 2 * kept
    return jnp.where((col % period) // 2 == row, 1.0, 0.0).astype(jnp.bfloat16)


def restrict(read, target, count, fine_plane, coarse_plane, rows, matrix, half, sums):
    kept = rows // 2
    parts = matrix.shape[0] // 128

    def body(j):
        pair = read(fine_plane + 2 * j) + read(fine_plane + 2 * j + 1)
        slot = j % 2
        for part in range(parts):
            half[slot, part, 0:rows, :] = pair[:, part * 128 : (part + 1) * 128]
        for part in range(parts):
            even = half[slot, part, pl.ds(0, kept, stride=2), :]
            odd = half[slot, part, pl.ds(1, kept, stride=2), :]
            sums[pl.ds(pl.multiple_of(j * kept, 8), kept), 128 * part : 128 * (part + 1)] = even + odd

    loop(0, count, body, 2)
    means = times(sums[0 : count * kept, 0 : 128 * parts], matrix)
    target[coarse_plane : coarse_plane + count, 0:kept, :] = means.reshape(count, kept, 128)


def grow(source, planes, rows, matrix, doubled):
    start, stop = planes
    count, parts = stop - start, matrix.shape[1] // 128
    wide = times(source[start:stop].reshape(count * rows, 128), matrix)
    for j in range(count):
        for part in range(parts):
            piece = wide[j * rows : (j + 1) * rows, 128 * part : 128 * (part + 1)]
            doubled[j, part, pl.ds(0, rows, stride=2), :] = piece
            doubled[j, part, pl.ds(1, rows, stride=2), :] = piece


def grown_plane(doubled, j, rows, parts):
    own = 2 * (rows - 8)
    upper = iota((8, 128), 0) < 4
    found = []
    for part in range(parts):
        tail = jnp.where(upper, doubled[j, part, own : own + 8, :], doubled[j, part, own + 8 : own + 16, :])
        found.append(jnp.concatenate([doubled[j, part, 0:own, :], tail], axis=0))
    return found[0] if parts == 1 else jnp.concatenate(found, axis=1)


def kernel(count_x, count_y, names, *refs):
    r = dict(zip(names, refs))
    gx, gy = lax.axis_index("gx"), lax.axis_index("gy")
    ring_x = 4
    ring_z = count_y // ring_x
    chip_x, chip_z = gy % ring_x, gy // ring_x

    def place(dx, dy):
        return ((gx + dx + count_x) % count_x, (gy + dy + count_y) % count_y)

    def along_x(d):
        return (gx, chip_z * ring_x + (chip_x + d) % ring_x)

    def along_z(d):
        return (gx, ((chip_z + d) % ring_z) * ring_x + chip_x)

    def along_gx(d):
        return ((gx + d) % count_x, gy)

    partners = [place(dx, dy) for dx, dy in STEPS]
    partners += [along_x(d) for d in range(1, ring_x)]
    partners += [along_z(d) for d in range(1, ring_z)]
    partners += [along_gx(d) for d in range(1, count_x)]

    barrier = pltpu.get_barrier_semaphore()
    for partner in partners:
        pl.semaphore_signal(barrier, inc=1, device_id=partner, device_id_type=MESH)

    def halves(whole, staged, first, store):
        copies = []
        for part in range(2):
            wide = whole.at[:, pl.ds(128 * part, 128)]
            pair = (staged.at[part], wide) if store else (wide, staged.at[part])
            copies.append(pltpu.make_async_copy(*pair, r["load"].at[first + part]))
        return copies

    loads_k = halves(r["coefficient"], r["k_in"], 0, False)
    loads_b = halves(r["right_side"], r["b_in"], 2, False)
    for copy in loads_k + loads_b:
        copy.start()

    def exchange(name, number, halo, depth):
        tag = f"{name}{number}"
        return Exchange(r[tag], r[tag + "_l"], r[tag + "_r"], r[tag + "_send"], r[tag + "_recv"], halo, depth)

    levels = []
    for number, (lanes, halo, depth_k, depth_b, depth_x) in enumerate(SHAPES):
        fields = [
            exchange("k", number, halo, depth_k),
            exchange("b", number, halo, depth_b),
            exchange("xh", number, halo, depth_x),
        ]
        fields += [r[f"{name}{number}"] for name in LOCAL]
        levels.append(Level(number, lanes, fields, gx, gy, (count_x, count_y)))
    l0, l1, l2 = levels
    l3 = Whole([r[f"{name}3"] for name in WHOLE])
    l4 = Deepest(count_x)

    def turn(staged, target):
        for y in range(l0.n):
            for part in range(2):
                lanes = pl.ds(128 * part, 128)
                target[l0.h + y, 0 : l0.x, lanes] = staged[part, pl.ds(y, l0.x, stride=l0.n), :]

    for copy in loads_k:
        copy.wait()
    turn(r["k_in"], r["k0"])
    for copy in loads_b:
        copy.wait()
    turn(r["b_in"], r["b0"])
    pl.semaphore_wait(barrier, len(partners))
    l0.k.start(place)
    l0.b.start(place)

    half, sums, doubled = r["half"], r["sums"], r["doubled"]
    k0, k1, k2 = r["k0"], r["k1"], r["k2"]
    to_1, to_2 = shrink_lanes(256, 128), shrink_lanes(128, 64)
    restrict(lambda p: k0[p, 0 : l0.x, :], k1, l1.n, l0.h, l1.h, l0.x, to_1, half, sums)
    l1.k.start(place)
    restrict(lambda p: k1[p, 0 : l1.x, :], k2, l2.n, l1.h, l2.h, l1.x, to_2, half, sums)
    l2.k.start(place)

    def small_block(read):
        row, col = iota((128, 128), 0), iota((128, 128), 1)
        matrix = jnp.where((row < 64) & (row // 2 == col % 32), 0.125, 0.0).astype(jnp.bfloat16)
        tile = (8, 128)
        mine = iota(tile, 1) // 32 == iota(tile, 0) // 2
        pairs = [read(l2.h + 2 * j) + read(l2.h + 2 * j + 1) for j in range(2)]
        means = times(jnp.concatenate(pairs, axis=0), matrix)
        found = jnp.zeros(tile, F32)
        for j in range(2):
            spread = jnp.where(mine, means[8 * j : 8 * j + 8], 0.0)
            line = jnp.sum(spread, axis=0, keepdims=True)
            found = jnp.where(iota(tile, 0) == 2 * chip_x + j, jnp.broadcast_to(line, tile), found)
        return found

    class Gather:
        def __init__(self, name, target):
            self.first, self.target = r[name + "_first"], target
            self.send, self.recv = r[name + "_send"], r[name + "_recv"]
            self.all = []

        def go(self, base, source, target, where, count):
            copies = []
            for d in range(1, count):
                copies.append(
                    pltpu.make_async_remote_copy(
                        src_ref=source,
                        dst_ref=target,
                        send_sem=self.send.at[base + d - 1],
                        recv_sem=self.recv.at[base + d - 1],
                        device_id=where(d),
                        device_id_type=MESH,
                    )
                )
            for copy in copies:
                copy.start()
            self.now = copies
            self.all += copies

        def along_x(self, tile):
            self.first[chip_x] = tile
            slot = self.first.at[chip_x]
            self.go(0, slot, slot, along_x, ring_x)

        def along_z(self):
            self.arrive()
            rows = pl.ds(pl.multiple_of(8 * chip_z + LOW, 8), 8)
            found = self.first[0]
            for slot in range(1, ring_x):
                found = found + self.first[slot]
            self.target[gx + 1, rows, :] = found
            part = self.target.at[gx + 1, rows]
            self.go(ring_x - 1, part, part, along_z, ring_z)

        def along_gx(self):
            self.arrive()
            part = self.target.at[gx + 1, pl.ds(LOW, 8 * ring_z)]
            self.go(ring_x + ring_z - 2, part, part, along_gx, count_x)

        def arrive(self):
            for copy in self.now:
                copy.wait_recv()

    gather_k, gather_b = Gather("gk", l3.k), Gather("gb", l3.b)
    gather_k.along_x(small_block(lambda p: k2[p, 0 : l2.x, :]))
    l3.blank()
    z0_3, z1_3 = r["z0_3"], r["z1_3"]
    for held in (z0_3, z1_3):
        held[0] = jnp.zeros((24, 128), F32)
        held[4] = jnp.zeros((24, 128), F32)
    grown3 = r["grown3"]
    for c in range(3):
        grown3[c, 0:LOW, :] = jnp.zeros((LOW, 128), F32)
        grown3[c, LOW + 8 * ring_z :, :] = jnp.zeros((HIGH, 128), F32)

    def ready(level):
        h, n, depth = level.h, level.n, level.k.depth
        level.k.arrive((2, 3))
        level.merge_k(h, h + n)
        level.faces(h, h + n)
        level.faces_y(h, h + n - 1)
        level.totals(h + 1, h + n - 1)
        level.k.arrive((0, 1, 4, 5, 6, 7))
        low, high = h - depth + 1, h + n + depth - 1
        level.merge_k(low, h)
        level.merge_k(h + n, high)
        level.mend_planes()
        level.faces(low, h)
        level.faces(h + n, high)
        level.faces_y(h - depth, h)
        level.faces_y(h + n - 1, high)
        level.totals(low, h + 1)
        level.totals(h + n - 1, high)

    def descend(level):
        h, n, depth = level.h, level.n, level.b.depth
        level.b.arrive(range(8))
        level.b.merge(h - depth + 1, h + n + depth - 1)
        level.first(h - depth, h + n + depth)
        level.second()

    def source_below(level, target, matrix):
        below = levels[levels.index(level) + 1]
        read = lambda p: level.residual(level.x2, p)[0 : level.x, :]
        restrict(read, target, below.n, level.h, below.h, level.x, matrix, half, sums)

    ready(l0)
    descend(l0)
    source_below(l0, r["b1"], shrink_lanes(256, 128))
    l1.b.start(place)
    l0.xh.start(place)
    gather_k.along_z()
    ready(l1)
    descend(l1)
    source_below(l1, r["b2"], shrink_lanes(128, 64))
    l2.b.start(place)
    l1.xh.start(place)
    gather_k.along_gx()
    ready(l2)
    descend(l2)
    gather_b.along_x(small_block(lambda p: l2.residual(l2.x2, p)[0 : l2.x, :]))
    l2.xh.start(place)

    def to_bottom(source, low):
        row, col = iota((128, 128), 0), iota((128, 128), 1)
        same_x = (row // 32) // 2 == (col % 32) // 16
        same_z = (row % 32) // 2 == col % 16
        matrix = jnp.where(same_x & same_z, 0.125, 0.0).astype(jnp.bfloat16)
        kept = 4 * ring_z
        pieces = []
        for g in range(count_x):
            even = source[g, pl.ds(low, kept, stride=2), :]
            odd = source[g, pl.ds(low + 1, kept, stride=2), :]
            pieces.append(even + odd)
        means = times(jnp.concatenate(pieces, axis=0), matrix)
        group = iota((8, 128), 1) // 32
        tiles = []
        for g in range(count_x):
            found = means[g * kept : g * kept + 8]
            for q in range(1, 4):
                found = jnp.where(group == q, means[g * kept + 8 * q : g * kept + 8 * q + 8], found)
            tiles.append(found)
        return tiles

    gather_k.arrive()
    l3.weights()
    l4.weights(to_bottom(l3.k.at[pl.ds(1, count_x)], LOW), r["w4"], r["inv4"])
    gather_b.along_z()
    gather_b.along_gx()
    gather_b.arrive()
    l3.down(r["left3"])
    deepest = l4.solve(to_bottom(r["left3"], 0), r["w4"], r["inv4"])
    tiles4 = r["tiles4"]
    tiles4[0] = l4.zero
    tiles4[count_x + 1] = l4.zero
    for g in range(count_x):
        tiles4[g + 1] = deepest[g]

    row, col = iota((128, 128), 0), iota((128, 128), 1)
    same = ((row % 32) // 16 == (col // 32) // 2) & (row % 16 == (col % 32) // 2)
    matrix_43 = jnp.where(same, 1.0, 0.0).astype(jnp.bfloat16)
    group = iota((8, 128), 1) // 32
    spread = [jnp.where(group == q, tiles4[gx + c], 0.0) for c in range(3) for q in range(4)]
    wide = times(jnp.concatenate(spread, axis=0), matrix_43)
    for c in range(3):
        piece = wide[32 * c : 32 * c + 32]
        grown3[c, pl.ds(LOW, 32, stride=2), :] = piece
        grown3[c, pl.ds(LOW + 1, 32, stride=2), :] = piece
    start = 8 * ((2 * gy + 4) // 8)
    answer = r["answer"]
    l3.up(gx, pl.multiple_of(start, 8), grown3, (z0_3, z1_3), answer)

    matrix_32 = jnp.where(iota((128, 128), 0) % 32 == (iota((128, 128), 1) % 64) // 2, 1.0, 0.0).astype(jnp.bfloat16)
    l2.xh.arrive(range(8))
    l2.xh.merge(l2.h - 3, l2.h + l2.n + 3)
    tile = (8, 128)
    own_group = iota(tile, 1) // 32 == iota(tile, 0) // 2
    first_half = iota(tile, 0) < 4
    spread = []
    for j in range(6):
        at = 6 + 2 * gy + j - start
        lower, own, upper = [jnp.broadcast_to(answer[c, pl.ds(at, 1), :], tile) for c in range(3)]
        spread.append(jnp.where(own_group, own, 0.0))
        spread.append(jnp.where(own_group, jnp.where(first_half, upper, lower), 0.0))
    wide = times(jnp.concatenate(spread, axis=0), matrix_32)
    l2.rows_ok = l2.row_ok()
    for p in range(12):
        l2.correct(p, wide[16 * (p // 2) : 16 * (p // 2) + 16])
    l2.third(1, 11)
    l2.fourth(2, 10, r["z2"])

    grow(r["z2"], (2, 10), 16, grow_lanes(64, 128), doubled)
    l1.xh.arrive(range(8))
    l1.xh.merge(l1.h - 3, l1.h + l1.n + 3)
    l1.rows_ok = l1.row_ok()

    def lift_1(j):
        grown = grown_plane(doubled, j, 16, 1)
        l1.correct(2 * j, grown)
        l1.correct(2 * j + 1, grown)

    loop(0, 8, lift_1, 2)
    l1.third(1, 15)
    l1.fourth(2, 14, r["z1out"])

    grow(r["z1out"], (2, 14), 24, grow_lanes(128, 256), doubled)
    l0.xh.arrive(range(8))
    l0.xh.merge(l0.h - 2, l0.h + l0.n + 2)
    l0.rows_ok = l0.row_ok()
    l0.correct(0, grown_plane(doubled, 0, 24, 2))

    def lift_0(j):
        grown = grown_plane(doubled, j, 24, 2)
        l0.correct(2 * j - 1, grown)
        l0.correct(2 * j, grown)

    loop(1, 11, lift_0)
    l0.correct(21, grown_plane(doubled, 11, 24, 2))
    l0.third(1, 21)
    l0.fourth(2, 20, l0.x2)

    def finish(y):
        p = l0.h + y
        left = l0.residual(l0.x2, p)
        for part in range(2):
            lanes = slice(128 * part, 128 * (part + 1))
            r["k_in"][part, pl.ds(y, l0.x, stride=l0.n), :] = l0.x2[p, 0 : l0.x, lanes]
            r["b_in"][part, pl.ds(y, l0.x, stride=l0.n), :] = left[0 : l0.x, lanes]

    loop(0, l0.n, finish, 2)
    stores = halves(r["solution"], r["k_in"], 4, True) + halves(r["residual"], r["b_in"], 6, True)
    for copy in stores:
        copy.start()
    for level in levels:
        for field in (level.k, level.b, level.xh):
            field.sent()
    for copy in gather_k.all + gather_b.all:
        copy.wait_send()
    for copy in stores:
        copy.wait()


SHAPES = ((256, 3, 3, 2, 3), (128, 4, 4, 3, 4), (64, 4, 4, 3, 4))
LOCAL = ("x1_", "x2_", "wx", "wy", "wz", "w", "inv", "z0_", "z1_")
WHOLE = ("k", "b", "x1_", "x2_", "wx", "wy", "wz", "w", "inv")


def per_device(count_x, count_y, right_side, coefficient):
    nx, ny, nz = right_side.shape
    vmem = lambda *shape: pltpu.VMEM(shape, F32)
    rows3 = 2 * count_y
    scratch = {
        "k_in": vmem(2, nx * ny, 128),
        "b_in": vmem(2, nx * ny, 128),
        "load": pltpu.SemaphoreType.DMA((8,)),
        "half": vmem(2, 2, nx, 128),
        "sums": vmem(nx * ny // 4, nz),
        "doubled": vmem(ny // 2 + 4, 2, nx + 16, 128),
        "z0_3": vmem(5, 24, 128),
        "z1_3": vmem(5, 24, 128),
        "left3": vmem(count_x, rows3, 128),
        "w4": vmem(6, count_x, 8, 128),
        "inv4": vmem(count_x, 8, 128),
        "tiles4": vmem(count_x + 2, 8, 128),
        "grown3": vmem(3, LOW + rows3 + HIGH, 128),
        "answer": vmem(3, 24, 128),
        "z2": vmem((ny >> 2) + 8, (nx >> 2) + 8, 128),
        "z1out": vmem((ny >> 1) + 8, (nx >> 1) + 8, 128),
    }
    for number, (lanes, halo, *_) in enumerate(SHAPES):
        rows, planes, width = nx >> number, ny >> number, max(128, lanes)
        full = (planes + 2 * halo, rows + 8, width)
        for name in ("k", "b", "xh"):
            tag = f"{name}{number}"
            scratch[tag] = vmem(*full)
            scratch[tag + "_l"] = vmem(full[0], 8, width)
            scratch[tag + "_r"] = vmem(full[0], 8, width)
            scratch[tag + "_send"] = pltpu.SemaphoreType.DMA((8,))
            scratch[tag + "_recv"] = pltpu.SemaphoreType.DMA((8,))
        for name in LOCAL:
            scratch[f"{name}{number}"] = vmem(*full)
    for name in WHOLE:
        scratch[f"{name}3"] = vmem(count_x + 2, LOW + rows3 + HIGH, 128)
    for name in ("gk", "gb"):
        scratch[name + "_first"] = vmem(4, 8, 128)
        scratch[name + "_send"] = pltpu.SemaphoreType.DMA((3 + count_y // 4 - 1 + count_x - 1,))
        scratch[name + "_recv"] = pltpu.SemaphoreType.DMA((3 + count_y // 4 - 1 + count_x - 1,))

    names = ["right_side", "coefficient", "solution", "residual"] + list(scratch)
    shape = jax.ShapeDtypeStruct((nx * ny, nz), F32)
    found = pl.pallas_call(
        functools.partial(kernel, count_x, count_y, names),
        out_shape=(shape, shape),
        in_specs=[pl.BlockSpec(memory_space=pl.ANY)] * 2,
        out_specs=(pl.BlockSpec(memory_space=pl.ANY),) * 2,
        scratch_shapes=list(scratch.values()),
        compiler_params=pltpu.CompilerParams(
            collective_id=0, has_side_effects=True, vmem_limit_bytes=56 << 20
        ),
        name="vcycle",
    )(right_side.reshape(nx * ny, nz), coefficient.reshape(nx * ny, nz))
    return tuple(value.reshape(nx, ny, nz) for value in found)


def solution(mesh):
    spec = P("gx", "gy", None)
    step = functools.partial(per_device, mesh.shape["gx"], mesh.shape["gy"])
    return jax.shard_map(step, mesh=mesh, in_specs=(spec, spec), out_specs=(spec, spec), check_vma=False)
```

time: 86.9 us -> 60 us (0.69)
  Pallas kernels: 79.1 us -> 56.5 us
  local copies, waits for them, and re-layouts: 6.95 us -> 2.72 us
    pallas_call x1, Pallas kernels: 79.1 us -> 56.5 us  [per_device(): pl.pallas_call(functools.partial(kernel, count_x, count_y, names), out_sh...]
    reshape x4 -> x0, local copies, waits for them, and re-layouts: 4.06 us -> none  [the longest x2 2.43 us: per_device(): join = lambda value: value.transpose(1, 0, 2).reshape(nx, ny, nz)]
    transpose x3 -> x0, local copies, waits for them, and re-layouts: 2.89 us -> none  [the longest x2 1.85 us: per_device(): join = lambda value: value.transpose(1, 0, 2).reshape(nx, ny, nz)]
    unnamed x4, local copies, waits for them, and re-layouts: 0.01 us -> 2.72 us
where the time goes in v2:
time: 60 us; the launch traced here: 59.8 us
  Pallas kernels  56.5 us (94%)
  local copies, waits for them, and re-layouts  2.72 us (5%)
  between operations  0.65 us (1%)
    pallas_call x1, Pallas kernels, per_device(): pl.pallas_call(functools.partial(kernel, count_x, count_y, names), out_sh...  56.5 us
    unnamed x4, local copies, waits for them, and re-layouts  2.72 us

profile of v2, /device:TPU:1, one launch (start us, length us, event | category | flops | bytes accessed | tf_op | source)
XLA Modules:
  0.0 59.8 jit_solution(874314063785563963)
XLA Ops:
  0.6 56.5 %vcycle.1 = (f32[512,256]{1,0:T(8,128)}, f32[512,256]{1,0:T(8,128)}) custom-call(f32[512,256]{1,0:T(8,128)} %bitcast.4, f32[512,256]{1,0:T(8,128)} %bitcast.5), custom_call_target="tpu_custom_call" | custom-call | tf_op jit(solution)/shard_map/vcycle/pallas_call | solution.py:905
  57.1 0.0 copy-start
  57.1 1.9 %copy.6 = f32[32,16,256]{2,1,0:T(8,128)} copy(f32[32,16,256]{2,1,0:T(8,128)} %bitcast.7) | data formatting | bytes 1048576
  59.0 0.0 copy-done
  59.0 0.8 %copy.7 = f32[32,16,256]{2,1,0:T(8,128)} copy(f32[32,16,256]{2,1,0:T(8,128)S(1)} %bitcast.6) | data formatting | bytes 1048576
Async XLA Ops:
  57.1 1.9 %copy-start = (f32[512,256]{1,0:T(8,128)S(1)}, f32[512,256]{1,0:T(8,128)}, u32[]{:S(2)}) copy-start(f32[512,256]{1,0:T(8,128)} %get-tuple-element.5) | copy-start | bytes 1572868

commit v3 on v2

--- a/solution.py
+++ b/solution.py
@@ -14,7 +14,8 @@
 COARSE_LO, COARSE_HI = 0.05, 2.0
 BOTTOM = 8
 
-STEPS = ((0, 1), (0, -1), (1, 0), (-1, 0), (1, 1), (1, -1), (-1, 1), (-1, -1))
+STEPS = ((1, 1), (1, -1), (-1, 1), (-1, -1), (0, 1), (0, -1), (1, 0), (-1, 0))
+ALONG_GX, ALONG_GY = (6, 7), (0, 1, 2, 3, 4, 5)
 
 
 def coefficients(low, high, sweeps):
@@ -71,12 +72,13 @@
 
 
 class Exchange:
-    def __init__(self, field, left, right, send, recv, halo, depth):
-        self.field, self.left, self.right = field, left, right
+    def __init__(self, field, landing, send, recv, halo, depth, corner):
+        self.field, self.wide = field, landing is None
+        self.left, self.right = (None, None) if self.wide else landing
         self.send, self.recv = send, recv
-        self.halo, self.depth = halo, depth
+        self.halo, self.depth, self.corner = halo, depth, corner
         self.planes = field.shape[0] - 2 * halo
-        self.rows = field.shape[1] - 8
+        self.rows = field.shape[1] - (16 if self.wide else 8)
 
     def copies(self, place):
         h, n, r, x = self.halo, self.planes, self.depth, self.rows
@@ -88,12 +90,15 @@
                 source = self.field.at[pl.ds(source_plane, r), pl.ds(0, x)]
                 target = self.field.at[pl.ds(target_plane, r), pl.ds(0, x)]
             else:
-                count = n if dy == 0 else r - 1
+                count = n if dy == 0 else self.corner
                 source_plane = h if dy <= 0 else h + n - count
                 target_plane = h if dy == 0 else (h - count if dy > 0 else h + n)
                 source = self.field.at[pl.ds(source_plane, count), pl.ds(x - 8 if dx > 0 else 0, 8)]
-                landing = self.left if dx > 0 else self.right
-                target = landing.at[pl.ds(target_plane, count)]
+                if self.wide:
+                    target = self.field.at[pl.ds(target_plane, count), pl.ds(x + 8 if dx > 0 else x, 8)]
+                else:
+                    landing = self.left if dx > 0 else self.right
+                    target = landing.at[pl.ds(target_plane, count)]
             found.append(
                 pltpu.make_async_remote_copy(
                     src_ref=source,
@@ -116,6 +121,8 @@
             self.started[number].wait_recv()
 
     def merge(self, start, stop):
+        if self.wide:
+            return
         x = self.rows
         shape = (8, self.field.shape[2])
 
@@ -132,6 +139,15 @@
         take_high = jnp.where(row == 0, at_high, 0) == 1
         take_low = jnp.where(row == 7, at_low, 0) == 1
         upper = row < 4
+
+        def ends(p):
+            high, low = self.field[p, x : x + 8, :], self.field[p, x + 8 :, :]
+            self.field[p, x : x + 8, :] = jnp.where(take_high, roll(self.field[p, x - 8 : x, :], 1, 0), high)
+            self.field[p, x + 8 :, :] = jnp.where(take_low, roll(self.field[p, 0:8, :], 7, 0), low)
+
+        if self.wide:
+            loop(start, stop, ends, 4)
+            return
 
         def body(p):
             tile = jnp.where(upper, self.right[p], self.left[p])
@@ -155,7 +171,7 @@
         self.h = self.k.halo
         self.n = self.k.planes
         self.x = self.k.rows
-        self.shape = (self.x + 8, 128 * ((lanes + 127) // 128))
+        self.shape = self.k.field.shape[1:]
         self.period = lanes
         self.unroll = 2 if number == 0 else 4
 
@@ -168,8 +184,9 @@
         row = iota(self.shape, 0)
         below = jnp.where(self.gx == 0, 1, 0)
         above = jnp.where(self.gx == self.count_x - 1, 1, 0)
-        bad_low = jnp.where(row >= self.x + 4, below, 0)
-        bad_high = jnp.where((row >= self.x) & (row < self.x + 4), above, 0)
+        middle = (self.x + self.shape[0]) // 2
+        bad_low = jnp.where(row >= middle, below, 0)
+        bad_high = jnp.where((row >= self.x) & (row < middle), above, 0)
         return (bad_low + bad_high) == 0
 
     def plane_ok(self, p):
@@ -231,14 +248,12 @@
         return found + wz * roll(own, -1, 1) + roll(wz * own, 1, 1)
 
     def first(self, start, stop):
-        b = self.b.field
-
         def body(p):
-            self.x1[p] = b[p] * self.inv[p] * (1.0 / (THETA * self.scale))
+            self.x1[p] = self.b[p] * self.inv[p] * (1.0 / (THETA * self.scale))
 
         loop(start, stop, body, self.unroll)
 
-    def second(self):
+    def second(self, margin):
         h, n, x = self.h, self.n, self.x
 
         def value(p):
@@ -246,21 +261,28 @@
             factor = 1.0 + MOMENTUM + STEP * (THETA - 1.0)
             return factor * own + STEP * (self.inv[p] * self.beside(self.x1, p))
 
-        def inner(p):
+        def plain(p):
+            self.x2[p] = value(p)
+
+        def kept(p):
             found = value(p)
             self.x2[p] = found
-            self.xh.field[p, 0:x, :] = found[0:x, :]
-
-        loop(h, h + n, inner, self.unroll)
-        for p in (h - 1, h + n):
-            self.x2[p] = value(p)
+            self.xh.field[p, 0:x, 0 : found.shape[1]] = found[0:x, :]
+
+        if self.xh is None:
+            loop(h - margin, h + n + margin, plain, self.unroll)
+            return
+        loop(h, h + n, kept, self.unroll)
+        for p in list(range(h - margin, h)) + list(range(h + n, h + n + margin)):
+            plain(p)
 
     def residual(self, field, p):
-        return self.b.field[p] - self.scale * (self.w[p] * field[p] - self.beside(field, p))
+        return self.b[p] - self.scale * (self.w[p] * field[p] - self.beside(field, p))
 
     def correct(self, p, grown):
         ok = self.rows_ok & self.plane_ok(p)
-        self.z0[p] = jnp.where(ok, self.xh.field[p] + grown, 0.0)
+        base = self.x2[p] if self.xh is None else self.xh.field[p, :, 0 : self.shape[1]]
+        self.z0[p] = jnp.where(ok, base + grown, 0.0)
 
     def third(self, start, stop):
         def body(p):
@@ -522,11 +544,11 @@
 
 
 def grown_plane(doubled, j, rows, parts):
-    own = 2 * (rows - 8)
+    own = 2 * (rows - 16)
     upper = iota((8, 128), 0) < 4
     found = []
     for part in range(parts):
-        tail = jnp.where(upper, doubled[j, part, own : own + 8, :], doubled[j, part, own + 8 : own + 16, :])
+        tail = jnp.where(upper, doubled[j, part, own : own + 8, :], doubled[j, part, own + 24 : own + 32, :])
         found.append(jnp.concatenate([doubled[j, part, 0:own, :], tail], axis=0))
     return found[0] if parts == 1 else jnp.concatenate(found, axis=1)
 
@@ -550,14 +572,11 @@
     def along_gx(d):
         return ((gx + d) % count_x, gy)
 
+    z_steps = [d for d in range(1, ring_z) if min(d, ring_z - d) <= 3]
     partners = [place(dx, dy) for dx, dy in STEPS]
     partners += [along_x(d) for d in range(1, ring_x)]
-    partners += [along_z(d) for d in range(1, ring_z)]
+    partners += [along_z(d) for d in z_steps]
     partners += [along_gx(d) for d in range(1, count_x)]
-
-    barrier = pltpu.get_barrier_semaphore()
-    for partner in partners:
-        pl.semaphore_signal(barrier, inc=1, device_id=partner, device_id_type=MESH)
 
     def halves(whole, staged, first, store):
         copies = []
@@ -571,18 +590,22 @@
     loads_b = halves(r["right_side"], r["b_in"], 2, False)
     for copy in loads_k + loads_b:
         copy.start()
+    barrier = pltpu.get_barrier_semaphore()
+    for partner in partners:
+        pl.semaphore_signal(barrier, inc=1, device_id=partner, device_id_type=MESH)
 
     def exchange(name, number, halo, depth):
         tag = f"{name}{number}"
-        return Exchange(r[tag], r[tag + "_l"], r[tag + "_r"], r[tag + "_send"], r[tag + "_recv"], halo, depth)
-
-    levels = []
+        if not depth:
+            return None
+        landing = (r[tag + "_l"], r[tag + "_r"]) if tag + "_l" in r else None
+        corner = depth if number == 2 else depth - 1
+        return Exchange(r[tag], landing, r[tag + "_send"], r[tag + "_recv"], halo, depth, corner)
+
+    levels, sources = [], []
     for number, (lanes, halo, depth_k, depth_b, depth_x) in enumerate(SHAPES):
-        fields = [
-            exchange("k", number, halo, depth_k),
-            exchange("b", number, halo, depth_b),
-            exchange("xh", number, halo, depth_x),
-        ]
+        sources.append(exchange("b", number, halo, depth_b))
+        fields = [exchange("k", number, halo, depth_k), r[f"b{number}"], exchange("xh", number, halo, depth_x)]
         fields += [r[f"{name}{number}"] for name in LOCAL]
         levels.append(Level(number, lanes, fields, gx, gy, (count_x, count_y)))
     l0, l1, l2 = levels
@@ -603,7 +626,7 @@
     turn(r["b_in"], r["b0"])
     pl.semaphore_wait(barrier, len(partners))
     l0.k.start(place)
-    l0.b.start(place)
+    sources[0].start(place)
 
     half, sums, doubled = r["half"], r["sums"], r["doubled"]
     k0, k1, k2 = r["k0"], r["k1"], r["k2"]
@@ -633,9 +656,9 @@
             self.send, self.recv = r[name + "_send"], r[name + "_recv"]
             self.all = []
 
-        def go(self, base, source, target, where, count):
+        def go(self, base, source, target, where, steps):
             copies = []
-            for d in range(1, count):
+            for d in steps:
                 copies.append(
                     pltpu.make_async_remote_copy(
                         src_ref=source,
@@ -654,7 +677,7 @@
         def along_x(self, tile):
             self.first[chip_x] = tile
             slot = self.first.at[chip_x]
-            self.go(0, slot, slot, along_x, ring_x)
+            self.go(0, slot, slot, along_x, range(1, ring_x))
 
         def along_z(self):
             self.arrive()
@@ -664,12 +687,12 @@
                 found = found + self.first[slot]
             self.target[gx + 1, rows, :] = found
             part = self.target.at[gx + 1, rows]
-            self.go(ring_x - 1, part, part, along_z, ring_z)
+            self.go(ring_x - 1, part, part, along_z, z_steps)
 
         def along_gx(self):
             self.arrive()
             part = self.target.at[gx + 1, pl.ds(LOW, 8 * ring_z)]
-            self.go(ring_x + ring_z - 2, part, part, along_gx, count_x)
+            self.go(ring_x + ring_z - 2, part, part, along_gx, range(1, count_x))
 
         def arrive(self):
             for copy in self.now:
@@ -678,6 +701,11 @@
     gather_k, gather_b = Gather("gk", l3.k), Gather("gb", l3.b)
     gather_k.along_x(small_block(lambda p: k2[p, 0 : l2.x, :]))
     l3.blank()
+    for d in range(1, ring_z):
+        if d not in z_steps:
+            unused = pl.ds(pl.multiple_of(8 * ((chip_z + d) % ring_z) + LOW, 8), 8)
+            l3.k[gx + 1, unused, :] = jnp.ones((8, 128), F32)
+            l3.b[gx + 1, unused, :] = jnp.zeros((8, 128), F32)
     z0_3, z1_3 = r["z0_3"], r["z1_3"]
     for held in (z0_3, z1_3):
         held[0] = jnp.zeros((24, 128), F32)
@@ -689,15 +717,15 @@
 
     def ready(level):
         h, n, depth = level.h, level.n, level.k.depth
-        level.k.arrive((2, 3))
+        level.k.arrive(ALONG_GX)
         level.merge_k(h, h + n)
         level.faces(h, h + n)
         level.faces_y(h, h + n - 1)
         level.totals(h + 1, h + n - 1)
-        level.k.arrive((0, 1, 4, 5, 6, 7))
+        level.k.arrive(ALONG_GY)
         low, high = h - depth + 1, h + n + depth - 1
-        level.merge_k(low, h)
-        level.merge_k(h + n, high)
+        level.merge_k(h - level.k.corner, h)
+        level.merge_k(h + n, h + n + level.k.corner)
         level.mend_planes()
         level.faces(low, h)
         level.faces(h + n, high)
@@ -706,33 +734,35 @@
         level.totals(low, h + 1)
         level.totals(h + n - 1, high)
 
-    def descend(level):
-        h, n, depth = level.h, level.n, level.b.depth
-        level.b.arrive(range(8))
-        level.b.merge(h - depth + 1, h + n + depth - 1)
+    def descend(level, source, depth):
+        h, n = level.h, level.n
+        if source is not None:
+            source.arrive(range(8))
+            source.merge(h - depth + 1, h + n + depth - 1)
         level.first(h - depth, h + n + depth)
-        level.second()
-
-    def source_below(level, target, matrix):
+        level.second(depth - 1)
+
+    def source_below(level, target, margin, rows, matrix):
         below = levels[levels.index(level) + 1]
-        read = lambda p: level.residual(level.x2, p)[0 : level.x, :]
-        restrict(read, target, below.n, level.h, below.h, level.x, matrix, half, sums)
+        read = lambda p: level.residual(level.x2, p)[0:rows, :]
+        count, fine = below.n + 2 * margin, level.h - 2 * margin
+        restrict(read, target, count, fine, below.h - margin, rows, matrix, half, sums)
 
     ready(l0)
-    descend(l0)
-    source_below(l0, r["b1"], shrink_lanes(256, 128))
-    l1.b.start(place)
+    descend(l0, sources[0], 2)
+    source_below(l0, r["b1"], 0, l0.x, shrink_lanes(256, 128))
+    sources[1].start(place)
     l0.xh.start(place)
     gather_k.along_z()
     ready(l1)
-    descend(l1)
-    source_below(l1, r["b2"], shrink_lanes(128, 64))
-    l2.b.start(place)
-    l1.xh.start(place)
+    descend(l1, sources[1], 6)
+    source_below(l1, r["b2"], 2, l1.x + 16, shrink_lanes(128, 64))
     gather_k.along_gx()
     ready(l2)
-    descend(l2)
+    descend(l2, None, 2)
     gather_b.along_x(small_block(lambda p: l2.residual(l2.x2, p)[0 : l2.x, :]))
+    for p in range(l2.h, l2.h + l2.n):
+        l2.xh.field[p, 0 : l2.x, 128:] = l2.x1[p, 0 : l2.x, :]
     l2.xh.start(place)
 
     def to_bottom(source, low):
@@ -761,6 +791,10 @@
     l4.weights(to_bottom(l3.k.at[pl.ds(1, count_x)], LOW), r["w4"], r["inv4"])
     gather_b.along_z()
     gather_b.along_gx()
+    for field in [level.k for level in levels] + sources[:2] + [l0.xh, l2.xh]:
+        field.sent()
+    for copy in gather_k.all:
+        copy.wait_send()
     gather_b.arrive()
     l3.down(r["left3"])
     deepest = l4.solve(to_bottom(r["left3"], 0), r["w4"], r["inv4"])
@@ -786,7 +820,7 @@
 
     matrix_32 = jnp.where(iota((128, 128), 0) % 32 == (iota((128, 128), 1) % 64) // 2, 1.0, 0.0).astype(jnp.bfloat16)
     l2.xh.arrive(range(8))
-    l2.xh.merge(l2.h - 3, l2.h + l2.n + 3)
+    l2.xh.merge(0, 2 * l2.h + l2.n)
     tile = (8, 128)
     own_group = iota(tile, 1) // 32 == iota(tile, 0) // 2
     first_half = iota(tile, 0) < 4
@@ -798,38 +832,38 @@
         spread.append(jnp.where(own_group, jnp.where(first_half, upper, lower), 0.0))
     wide = times(jnp.concatenate(spread, axis=0), matrix_32)
     l2.rows_ok = l2.row_ok()
+    for p in range(1, 11):
+        l2.x1[p] = jnp.where(l2.rows_ok & l2.plane_ok(p), l2.xh.field[p, :, 128:], 0.0)
     for p in range(12):
         l2.correct(p, wide[16 * (p // 2) : 16 * (p // 2) + 16])
     l2.third(1, 11)
     l2.fourth(2, 10, r["z2"])
 
     grow(r["z2"], (2, 10), 16, grow_lanes(64, 128), doubled)
-    l1.xh.arrive(range(8))
-    l1.xh.merge(l1.h - 3, l1.h + l1.n + 3)
     l1.rows_ok = l1.row_ok()
 
     def lift_1(j):
-        grown = grown_plane(doubled, j, 16, 1)
-        l1.correct(2 * j, grown)
-        l1.correct(2 * j + 1, grown)
+        grown = doubled[j, 0, 0 : l1.x + 16, :]
+        l1.correct(l1.h - 4 + 2 * j, grown)
+        l1.correct(l1.h - 3 + 2 * j, grown)
 
     loop(0, 8, lift_1, 2)
-    l1.third(1, 15)
-    l1.fourth(2, 14, r["z1out"])
-
-    grow(r["z1out"], (2, 14), 24, grow_lanes(128, 256), doubled)
+    l1.third(l1.h - 3, l1.h + l1.n + 3)
+    l1.fourth(l1.h - 2, l1.h + l1.n + 2, r["z1out"])
+
+    grow(r["z1out"], (l1.h - 2, l1.h + l1.n + 2), 32, grow_lanes(128, 256), doubled)
     l0.xh.arrive(range(8))
     l0.xh.merge(l0.h - 2, l0.h + l0.n + 2)
     l0.rows_ok = l0.row_ok()
-    l0.correct(0, grown_plane(doubled, 0, 24, 2))
+    l0.correct(0, grown_plane(doubled, 0, 32, 2))
 
     def lift_0(j):
-        grown = grown_plane(doubled, j, 24, 2)
+        grown = grown_plane(doubled, j, 32, 2)
         l0.correct(2 * j - 1, grown)
         l0.correct(2 * j, grown)
 
     loop(1, 11, lift_0)
-    l0.correct(21, grown_plane(doubled, 11, 24, 2))
+    l0.correct(21, grown_plane(doubled, 11, 32, 2))
     l0.third(1, 21)
     l0.fourth(2, 20, l0.x2)
 
@@ -845,16 +879,13 @@
     stores = halves(r["solution"], r["k_in"], 4, True) + halves(r["residual"], r["b_in"], 6, True)
     for copy in stores:
         copy.start()
-    for level in levels:
-        for field in (level.k, level.b, level.xh):
-            field.sent()
-    for copy in gather_k.all + gather_b.all:
+    for copy in gather_b.all:
         copy.wait_send()
     for copy in stores:
         copy.wait()
 
 
-SHAPES = ((256, 3, 3, 2, 3), (128, 4, 4, 3, 4), (64, 4, 4, 3, 4))
+SHAPES = ((256, 3, 3, 2, 3), (128, 7, 7, 6, 0), (64, 4, 4, 0, 4))
 LOCAL = ("x1_", "x2_", "wx", "wy", "wz", "w", "inv", "z0_", "z1_")
 WHOLE = ("k", "b", "x1_", "x2_", "wx", "wy", "wz", "w", "inv")
 
@@ -869,7 +900,7 @@
         "load": pltpu.SemaphoreType.DMA((8,)),
         "half": vmem(2, 2, nx, 128),
         "sums": vmem(nx * ny // 4, nz),
-        "doubled": vmem(ny // 2 + 4, 2, nx + 16, 128),
+        "doubled": vmem(ny // 2 + 4, 2, nx + 32, 128),
         "z0_3": vmem(5, 24, 128),
         "z1_3": vmem(5, 24, 128),
         "left3": vmem(count_x, rows3, 128),
@@ -879,16 +910,22 @@
         "grown3": vmem(3, LOW + rows3 + HIGH, 128),
         "answer": vmem(3, 24, 128),
         "z2": vmem((ny >> 2) + 8, (nx >> 2) + 8, 128),
-        "z1out": vmem((ny >> 1) + 8, (nx >> 1) + 8, 128),
+        "z1out": vmem((ny >> 1) + 14, (nx >> 1) + 16, 128),
     }
-    for number, (lanes, halo, *_) in enumerate(SHAPES):
+    for number, (lanes, halo, *depths) in enumerate(SHAPES):
         rows, planes, width = nx >> number, ny >> number, max(128, lanes)
-        full = (planes + 2 * halo, rows + 8, width)
-        for name in ("k", "b", "xh"):
+        wide = number == 1
+        full = (planes + 2 * halo, rows + (16 if wide else 8), width)
+        scratch[f"b{number}"] = vmem(*full)
+        for name, depth in zip(("k", "b", "xh"), depths):
+            if not depth:
+                continue
             tag = f"{name}{number}"
-            scratch[tag] = vmem(*full)
-            scratch[tag + "_l"] = vmem(full[0], 8, width)
-            scratch[tag + "_r"] = vmem(full[0], 8, width)
+            lanes_sent = 2 * width if tag == "xh2" else width
+            scratch[tag] = vmem(*full[:2], lanes_sent)
+            if not wide:
+                scratch[tag + "_l"] = vmem(full[0], 8, lanes_sent)
+                scratch[tag + "_r"] = vmem(full[0], 8, lanes_sent)
             scratch[tag + "_send"] = pltpu.SemaphoreType.DMA((8,))
             scratch[tag + "_recv"] = pltpu.SemaphoreType.DMA((8,))
         for name in LOCAL:

time: 60 us -> 58.6 us (0.977)
  Pallas kernels: 56.5 us -> 55.1 us
    pallas_call x1, Pallas kernels: 56.5 us -> 55.1 us  [per_device(): pl.pallas_call(functools.partial(kernel, count_x, count_y, names), out_sh...]
where the time goes in v3:
time: 58.6 us; the launch traced here: 58.4 us
  Pallas kernels  55.1 us (94%)
  local copies, waits for them, and re-layouts  2.72 us (5%)
  between operations  0.65 us (1%)
    pallas_call x1, Pallas kernels, per_device(): pl.pallas_call(functools.partial(kernel, count_x, count_y, names), out_sh...  55.1 us
    unnamed x4, local copies, waits for them, and re-layouts  2.72 us

profile of v3, /device:TPU:1, one launch (start us, length us, event | category | flops | bytes accessed | tf_op | source)
XLA Modules:
  0.0 58.4 jit_solution(2927996138024312779)
XLA Ops:
  0.6 55.1 %vcycle.1 = (f32[512,256]{1,0:T(8,128)}, f32[512,256]{1,0:T(8,128)}) custom-call(f32[512,256]{1,0:T(8,128)} %bitcast.4, f32[512,256]{1,0:T(8,128)} %bitcast.5), custom_call_target="tpu_custom_call" | custom-call | tf_op jit(solution)/shard_map/vcycle/pallas_call | solution.py:942
  55.7 0.0 copy-start
  55.7 1.9 %copy.6 = f32[32,16,256]{2,1,0:T(8,128)} copy(f32[32,16,256]{2,1,0:T(8,128)} %bitcast.7) | data formatting | bytes 1048576
  57.6 0.0 copy-done
  57.6 0.8 %copy.7 = f32[32,16,256]{2,1,0:T(8,128)} copy(f32[32,16,256]{2,1,0:T(8,128)S(1)} %bitcast.6) | data formatting | bytes 1048576
Async XLA Ops:
  55.7 1.9 %copy-start = (f32[512,256]{1,0:T(8,128)S(1)}, f32[512,256]{1,0:T(8,128)}, u32[]{:S(2)}) copy-start(f32[512,256]{1,0:T(8,128)} %get-tuple-element.5) | copy-start | bytes 1572868

commit v4 on v3

--- a/solution.py
+++ b/solution.py
@@ -72,7 +72,8 @@
 
 
 class Exchange:
-    def __init__(self, field, landing, send, recv, halo, depth, corner):
+    def __init__(self, field, landing, send, recv, halo, depth, corner, skip=0):
+        self.skip = skip
         self.field, self.wide = field, landing is None
         self.left, self.right = (None, None) if self.wide else landing
         self.send, self.recv = send, recv
@@ -82,13 +83,14 @@
 
     def copies(self, place):
         h, n, r, x = self.halo, self.planes, self.depth, self.rows
-        found = []
+        found, self.tiles = [], 0
         for number, (dx, dy) in enumerate(STEPS):
             if dx == 0:
-                source_plane = h + n - r if dy > 0 else h
-                target_plane = h - r if dy > 0 else h + n
-                source = self.field.at[pl.ds(source_plane, r), pl.ds(0, x)]
-                target = self.field.at[pl.ds(target_plane, r), pl.ds(0, x)]
+                count, skip = r - self.skip, self.skip
+                source_plane = h + n - r if dy > 0 else h + skip
+                target_plane = h - r if dy > 0 else h + n + skip
+                source = self.field.at[pl.ds(source_plane, count), pl.ds(0, x)]
+                target = self.field.at[pl.ds(target_plane, count), pl.ds(0, x)]
             else:
                 count = n if dy == 0 else self.corner
                 source_plane = h if dy <= 0 else h + n - count
@@ -99,11 +101,12 @@
                 else:
                     landing = self.left if dx > 0 else self.right
                     target = landing.at[pl.ds(target_plane, count)]
+            self.tiles += source.shape[0] * source.shape[1] * source.shape[2] // 1024
             found.append(
                 pltpu.make_async_remote_copy(
                     src_ref=source,
                     dst_ref=target,
-                    send_sem=self.send.at[number],
+                    send_sem=self.send.at[0],
                     recv_sem=self.recv.at[number],
                     device_id=place(dx, dy),
                     device_id_type=MESH,
@@ -156,9 +159,9 @@
 
         loop(start, stop, body, 4)
 
-    def sent(self):
-        for copy in self.started:
-            copy.wait_send()
+    def sent(self, idle):
+        whole = idle.at[pl.ds(0, self.tiles)]
+        pltpu.make_async_copy(whole, whole, self.send.at[0]).wait()
 
 
 class Level:
@@ -218,6 +221,39 @@
 
         loop(start, stop, body, self.unroll)
 
+    def faces_inside(self):
+        k, h, n, x = self.k.field, self.h, self.n, self.x
+        last = self.lane()[0:x] == self.period - 1
+
+        def body(p):
+            own = k[p, 0:x, :]
+            self.wx[p, 0:x, :] = harmonic(own, roll(own, -1, 0))
+            self.wz[p, 0:x, :] = jnp.where(last, 0.0, harmonic(own, roll(own, -1, 1)))
+
+        def along(p):
+            self.wy[p, 0:x, :] = harmonic(k[p, 0:x, :], k[p + 1, 0:x, :])
+
+        loop(h, h + n, body, self.unroll)
+        loop(h, h + n - 1, along, self.unroll)
+
+    def faces_edge(self):
+        k, h, n, x = self.k.field, self.h, self.n, self.x
+        last = self.lane()[0:8] == self.period - 1
+        inner = iota((8, self.shape[1]), 0) < 7
+        after = lambda own, following: jnp.where(inner, roll(own, -1, 0), roll(following, -1, 0))
+
+        def body(p):
+            first, end, halo = k[p, 0:8, :], k[p, x - 8 : x, :], k[p, x:, :]
+            self.wx[p, x - 8 : x, :] = harmonic(end, after(end, halo))
+            self.wx[p, x:, :] = harmonic(halo, after(halo, first))
+            self.wz[p, x:, :] = jnp.where(last, 0.0, harmonic(halo, roll(halo, -1, 1)))
+
+        def along(p):
+            self.wy[p, x:, :] = harmonic(k[p, x:, :], k[p + 1, x:, :])
+
+        loop(h, h + n, body, 4)
+        loop(h, h + n - 1, along, 4)
+
     def faces_y(self, start, stop):
         k = self.k.field
 
@@ -267,21 +303,24 @@
         def kept(p):
             found = value(p)
             self.x2[p] = found
-            self.xh.field[p, 0:x, 0 : found.shape[1]] = found[0:x, :]
+            if self.lanes < 128:
+                first = iota(found.shape, 1) < self.lanes
+                found = jnp.where(first, found, self.x1[p])
+            self.xh.field[p, 0:x, :] = found[0:x, :]
 
         if self.xh is None:
             loop(h - margin, h + n + margin, plain, self.unroll)
             return
         loop(h, h + n, kept, self.unroll)
         for p in list(range(h - margin, h)) + list(range(h + n, h + n + margin)):
-            plain(p)
+            plain(p) if self.xh.skip == 0 else kept(p)
 
     def residual(self, field, p):
         return self.b[p] - self.scale * (self.w[p] * field[p] - self.beside(field, p))
 
     def correct(self, p, grown):
         ok = self.rows_ok & self.plane_ok(p)
-        base = self.x2[p] if self.xh is None else self.xh.field[p, :, 0 : self.shape[1]]
+        base = self.x2[p] if self.xh is None or self.lanes < 128 else self.xh.field[p]
         self.z0[p] = jnp.where(ok, base + grown, 0.0)
 
     def third(self, start, stop):
@@ -600,7 +639,7 @@
             return None
         landing = (r[tag + "_l"], r[tag + "_r"]) if tag + "_l" in r else None
         corner = depth if number == 2 else depth - 1
-        return Exchange(r[tag], landing, r[tag + "_send"], r[tag + "_recv"], halo, depth, corner)
+        return Exchange(r[tag], landing, r[tag + "_send"], r[tag + "_recv"], halo, depth, corner, 1 if tag == "xh0" else 0)
 
     levels, sources = [], []
     for number, (lanes, halo, depth_k, depth_b, depth_x) in enumerate(SHAPES):
@@ -634,7 +673,6 @@
     restrict(lambda p: k0[p, 0 : l0.x, :], k1, l1.n, l0.h, l1.h, l0.x, to_1, half, sums)
     l1.k.start(place)
     restrict(lambda p: k1[p, 0 : l1.x, :], k2, l2.n, l1.h, l2.h, l1.x, to_2, half, sums)
-    l2.k.start(place)
 
     def small_block(read):
         row, col = iota((128, 128), 0), iota((128, 128), 1)
@@ -651,61 +689,79 @@
         return found
 
     class Gather:
-        def __init__(self, name, target):
-            self.first, self.target = r[name + "_first"], target
+        def __init__(self, name, target, eager):
+            self.first, self.target, self.eager = r[name + "_first"], target, eager
             self.send, self.recv = r[name + "_send"], r[name + "_recv"]
-            self.all = []
-
-        def go(self, base, source, target, where, steps):
+            self.tiles_sent, self.tiles_last = 0, 0
+
+        def go(self, sems, source, target, where, steps):
             copies = []
             for d in steps:
                 copies.append(
                     pltpu.make_async_remote_copy(
                         src_ref=source,
                         dst_ref=target,
-                        send_sem=self.send.at[base + d - 1],
-                        recv_sem=self.recv.at[base + d - 1],
+                        send_sem=self.send.at[0],
+                        recv_sem=self.recv.at[sems(d)],
                         device_id=where(d),
                         device_id_type=MESH,
                     )
                 )
             for copy in copies:
                 copy.start()
-            self.now = copies
-            self.all += copies
+            self.tiles_sent += len(copies) * (source.shape[0] // 8)
+            return copies
 
         def along_x(self, tile):
             self.first[chip_x] = tile
             slot = self.first.at[chip_x]
-            self.go(0, slot, slot, along_x, range(1, ring_x))
+            self.near = self.go(lambda d: d, slot, slot, along_x, range(1, ring_x))
+
+        def part(self, d):
+            rows = pl.ds(pl.multiple_of(8 * ((chip_z + ring_z - d) % ring_z) + LOW, 8), 8)
+            return self.target.at[gx + 1, rows]
+
+        def pass_on(self, part):
+            self.go(lambda d: 0, part, part, along_gx, range(1, count_x))
+            self.tiles_last += (count_x - 1) * (part.shape[0] // 8)
 
         def along_z(self):
-            self.arrive()
-            rows = pl.ds(pl.multiple_of(8 * chip_z + LOW, 8), 8)
+            for copy in self.near:
+                copy.wait_recv()
             found = self.first[0]
             for slot in range(1, ring_x):
                 found = found + self.first[slot]
-            self.target[gx + 1, rows, :] = found
-            part = self.target.at[gx + 1, rows]
-            self.go(ring_x - 1, part, part, along_z, z_steps)
+            tile = self.part(0)
+            tile[...] = found
+            self.far = self.go(lambda d: ring_x - 1 + d, tile, tile, along_z, z_steps)
+            if self.eager:
+                self.pass_on(tile)
 
         def along_gx(self):
-            self.arrive()
-            part = self.target.at[gx + 1, pl.ds(LOW, 8 * ring_z)]
-            self.go(ring_x + ring_z - 2, part, part, along_gx, range(1, count_x))
+            for d, copy in sorted(zip(z_steps, self.far), key=lambda pair: min(pair[0], ring_z - pair[0])):
+                copy.wait_recv()
+                if self.eager:
+                    self.pass_on(self.part(d))
+            if not self.eager:
+                self.pass_on(self.target.at[gx + 1, pl.ds(LOW, 8 * ring_z)])
 
         def arrive(self):
-            for copy in self.now:
-                copy.wait_recv()
-
-    gather_k, gather_b = Gather("gk", l3.k), Gather("gb", l3.b)
+            whole = r["idle"].at[pl.ds(0, self.tiles_last)]
+            pltpu.make_async_copy(whole, whole, self.recv.at[0]).wait()
+
+        def sent(self):
+            whole = r["idle"].at[pl.ds(0, self.tiles_sent)]
+            pltpu.make_async_copy(whole, whole, self.send.at[0]).wait()
+
+    gather_k, gather_b = Gather("gk", l3.k, False), Gather("gb", l3.b, True)
     gather_k.along_x(small_block(lambda p: k2[p, 0 : l2.x, :]))
     l3.blank()
     for d in range(1, ring_z):
         if d not in z_steps:
             unused = pl.ds(pl.multiple_of(8 * ((chip_z + d) % ring_z) + LOW, 8), 8)
             l3.k[gx + 1, unused, :] = jnp.ones((8, 128), F32)
-            l3.b[gx + 1, unused, :] = jnp.zeros((8, 128), F32)
+            for g in range(1, count_x + 1):
+                l3.b[g, unused, :] = jnp.zeros((8, 128), F32)
     z0_3, z1_3 = r["z0_3"], r["z1_3"]
     for held in (z0_3, z1_3):
         held[0] = jnp.zeros((24, 128), F32)
@@ -715,13 +771,21 @@
         grown3[c, 0:LOW, :] = jnp.zeros((LOW, 128), F32)
         grown3[c, LOW + 8 * ring_z :, :] = jnp.zeros((HIGH, 128), F32)
 
-    def ready(level):
+    def ready(level, between=None):
         h, n, depth = level.h, level.n, level.k.depth
-        level.k.arrive(ALONG_GX)
-        level.merge_k(h, h + n)
-        level.faces(h, h + n)
-        level.faces_y(h, h + n - 1)
+        if level.k.wide:
+            level.k.arrive(ALONG_GX)
+            level.merge_k(h, h + n)
+            level.faces(h, h + n)
+            level.faces_y(h, h + n - 1)
+        else:
+            level.faces_inside()
+            level.k.arrive(ALONG_GX)
+            level.merge_k(h, h + n)
+            level.faces_edge()
         level.totals(h + 1, h + n - 1)
+        if between is not None:
+            between()
         level.k.arrive(ALONG_GY)
         low, high = h - depth + 1, h + n + depth - 1
         level.merge_k(h - level.k.corner, h)
@@ -748,23 +812,18 @@
         count, fine = below.n + 2 * margin, level.h - 2 * margin
         restrict(read, target, count, fine, below.h - margin, rows, matrix, half, sums)
 
-    ready(l0)
+    ready(l0, gather_k.along_z)
     descend(l0, sources[0], 2)
     source_below(l0, r["b1"], 0, l0.x, shrink_lanes(256, 128))
     sources[1].start(place)
-    l0.xh.start(place)
-    gather_k.along_z()
+    gather_k.along_gx()
+    l2.k.start(place)
     ready(l1)
     descend(l1, sources[1], 6)
     source_below(l1, r["b2"], 2, l1.x + 16, shrink_lanes(128, 64))
-    gather_k.along_gx()
     ready(l2)
     descend(l2, None, 2)
     gather_b.along_x(small_block(lambda p: l2.residual(l2.x2, p)[0 : l2.x, :]))
-    for p in range(l2.h, l2.h + l2.n):
-        l2.xh.field[p, 0 : l2.x, 128:] = l2.x1[p, 0 : l2.x, :]
-    l2.xh.start(place)
-
     def to_bottom(source, low):
         row, col = iota((128, 128), 0), iota((128, 128), 1)
         same_x = (row // 32) // 2 == (col % 32) // 16
@@ -788,13 +847,14 @@
 
     gather_k.arrive()
     l3.weights()
+    gather_b.along_z()
     l4.weights(to_bottom(l3.k.at[pl.ds(1, count_x)], LOW), r["w4"], r["inv4"])
-    gather_b.along_z()
     gather_b.along_gx()
-    for field in [level.k for level in levels] + sources[:2] + [l0.xh, l2.xh]:
-        field.sent()
-    for copy in gather_k.all:
-        copy.wait_send()
+    l2.xh.start(place)
+    l0.xh.start(place)
+    for field in [level.k for level in levels] + sources[:2]:
+        field.sent(r["idle"])
+    gather_k.sent()
     gather_b.arrive()
     l3.down(r["left3"])
     deepest = l4.solve(to_bottom(r["left3"], 0), r["w4"], r["inv4"])
@@ -832,9 +892,12 @@
         spread.append(jnp.where(own_group, jnp.where(first_half, upper, lower), 0.0))
     wide = times(jnp.concatenate(spread, axis=0), matrix_32)
     l2.rows_ok = l2.row_ok()
-    for p in range(1, 11):
-        l2.x1[p] = jnp.where(l2.rows_ok & l2.plane_ok(p), l2.xh.field[p, :, 128:], 0.0)
+    low_lanes = iota(l2.shape, 1) < 64
     for p in range(12):
+        both = l2.xh.field[p]
+        turned = roll(both, 64, 1)
+        l2.x1[p] = jnp.where(l2.rows_ok & l2.plane_ok(p), jnp.where(low_lanes, turned, both), 0.0)
+        l2.x2[p] = jnp.where(low_lanes, both, turned)
         l2.correct(p, wide[16 * (p // 2) : 16 * (p // 2) + 16])
     l2.third(1, 11)
     l2.fourth(2, 10, r["z2"])
@@ -867,20 +930,22 @@
     l0.third(1, 21)
     l0.fourth(2, 20, l0.x2)
 
-    def finish(y):
-        p = l0.h + y
-        left = l0.residual(l0.x2, p)
+    def turn_back(staged, y, value):
         for part in range(2):
             lanes = slice(128 * part, 128 * (part + 1))
-            r["k_in"][part, pl.ds(y, l0.x, stride=l0.n), :] = l0.x2[p, 0 : l0.x, lanes]
-            r["b_in"][part, pl.ds(y, l0.x, stride=l0.n), :] = left[0 : l0.x, lanes]
-
-    loop(0, l0.n, finish, 2)
-    stores = halves(r["solution"], r["k_in"], 4, True) + halves(r["residual"], r["b_in"], 6, True)
+            staged[part, pl.ds(y, l0.x, stride=l0.n), :] = value[0 : l0.x, lanes]
+
+    loop(0, l0.n, lambda y: turn_back(r["k_in"], y, l0.x2[l0.h + y]), 4)
+    stores = halves(r["solution"], r["k_in"], 4, True)
     for copy in stores:
         copy.start()
-    for copy in gather_b.all:
-        copy.wait_send()
+    loop(0, l0.n, lambda y: turn_back(r["b_in"], y, l0.residual(l0.x2, l0.h + y)), 2)
+    for copy in halves(r["residual"], r["b_in"], 6, True):
+        copy.start()
+        stores.append(copy)
+    gather_b.sent()
+    l2.xh.sent(r["idle"])
+    l0.xh.sent(r["idle"])
     for copy in stores:
         copy.wait()
 
@@ -899,6 +964,7 @@
         "b_in": vmem(2, nx * ny, 128),
         "load": pltpu.SemaphoreType.DMA((8,)),
         "half": vmem(2, 2, nx, 128),
+        "idle": vmem(256, 8, 128),
         "sums": vmem(nx * ny // 4, nz),
         "doubled": vmem(ny // 2 + 4, 2, nx + 32, 128),
         "z0_3": vmem(5, 24, 128),
@@ -921,12 +987,11 @@
             if not depth:
                 continue
             tag = f"{name}{number}"
-            lanes_sent = 2 * width if tag == "xh2" else width
-            scratch[tag] = vmem(*full[:2], lanes_sent)
+            scratch[tag] = vmem(*full)
             if not wide:
-                scratch[tag + "_l"] = vmem(full[0], 8, lanes_sent)
-                scratch[tag + "_r"] = vmem(full[0], 8, lanes_sent)
-            scratch[tag + "_send"] = pltpu.SemaphoreType.DMA((8,))
+                scratch[tag + "_l"] = vmem(full[0], 8, width)
+                scratch[tag + "_r"] = vmem(full[0], 8, width)
+            scratch[tag + "_send"] = pltpu.SemaphoreType.DMA((1,))
             scratch[tag + "_recv"] = pltpu.SemaphoreType.DMA((8,))
         for name in LOCAL:
             scratch[f"{name}{number}"] = vmem(*full)
@@ -934,8 +999,8 @@
         scratch[f"{name}3"] = vmem(count_x + 2, LOW + rows3 + HIGH, 128)
     for name in ("gk", "gb"):
         scratch[name + "_first"] = vmem(4, 8, 128)
-        scratch[name + "_send"] = pltpu.SemaphoreType.DMA((3 + count_y // 4 - 1 + count_x - 1,))
-        scratch[name + "_recv"] = pltpu.SemaphoreType.DMA((3 + count_y // 4 - 1 + count_x - 1,))
+        scratch[name + "_send"] = pltpu.SemaphoreType.DMA((1,))
+        scratch[name + "_recv"] = pltpu.SemaphoreType.DMA((4 + count_y // 4,))
 
     names = ["right_side", "coefficient", "solution", "residual"] + list(scratch)
     shape = jax.ShapeDtypeStruct((nx * ny, nz), F32)

time: 58.6 us -> 55.8 us (0.952)
  Pallas kernels: 55.1 us -> 52.3 us
    pallas_call x1, Pallas kernels: 55.1 us -> 52.3 us  [per_device(): pl.pallas_call(functools.partial(kernel, count_x, count_y, names), out_sh...]
where the time goes in v4:
time: 55.8 us; the launch traced here: 55.6 us
  Pallas kernels  52.3 us (94%)
  local copies, waits for them, and re-layouts  2.72 us (5%)
  between operations  0.65 us (1%)
    pallas_call x1, Pallas kernels, per_device(): pl.pallas_call(functools.partial(kernel, count_x, count_y, names), out_sh...  52.3 us
    unnamed x4, local copies, waits for them, and re-layouts  2.72 us

profile of v4, /device:TPU:1, one launch (start us, length us, event | category | flops | bytes accessed | tf_op | source)
XLA Modules:
  0.0 55.6 jit_solution(11911460986352381049)
XLA Ops:
  0.6 52.3 %vcycle.1 = (f32[512,256]{1,0:T(8,128)}, f32[512,256]{1,0:T(8,128)}) custom-call(f32[512,256]{1,0:T(8,128)} %bitcast.4, f32[512,256]{1,0:T(8,128)} %bitcast.5), custom_call_target="tpu_custom_call" | custom-call | tf_op jit(solution)/shard_map/vcycle/pallas_call | solution.py:1007
  52.9 0.0 copy-start
  52.9 1.9 %copy.6 = f32[32,16,256]{2,1,0:T(8,128)} copy(f32[32,16,256]{2,1,0:T(8,128)} %bitcast.7) | data formatting | bytes 1048576
  54.8 0.0 copy-done
  54.9 0.8 %copy.7 = f32[32,16,256]{2,1,0:T(8,128)} copy(f32[32,16,256]{2,1,0:T(8,128)S(1)} %bitcast.6) | data formatting | bytes 1048576
Async XLA Ops:
  52.9 1.9 %copy-start = (f32[512,256]{1,0:T(8,128)S(1)}, f32[512,256]{1,0:T(8,128)}, u32[]{:S(2)}) copy-start(f32[512,256]{1,0:T(8,128)} %get-tuple-element.5) | copy-start | bytes 1572868

commit v5 on v4

--- a/solution.py
+++ b/solution.py
@@ -567,14 +567,14 @@
             sums[pl.ds(pl.multiple_of(j * kept, 8), kept), 128 * part : 128 * (part + 1)] = even + odd
 
     loop(0, count, body, 2)
-    means = times(sums[0 : count * kept, 0 : 128 * parts], matrix)
+    means = times(sums[0 : count * kept, 0 : 128 * parts], matrix[...])
     target[coarse_plane : coarse_plane + count, 0:kept, :] = means.reshape(count, kept, 128)
 
 
 def grow(source, planes, rows, matrix, doubled):
     start, stop = planes
     count, parts = stop - start, matrix.shape[1] // 128
-    wide = times(source[start:stop].reshape(count * rows, 128), matrix)
+    wide = times(source[start:stop].reshape(count * rows, 128), matrix[...])
     for j in range(count):
         for part in range(parts):
             piece = wide[j * rows : (j + 1) * rows, 128 * part : 128 * (part + 1)]
@@ -657,6 +657,20 @@
                 lanes = pl.ds(128 * part, 128)
                 target[l0.h + y, 0 : l0.x, lanes] = staged[part, pl.ds(y, l0.x, stride=l0.n), :]
 
+    square = (128, 128)
+    row, col = iota(square, 0), iota(square, 1)
+    same_x, same_z = (row // 32) // 2 == (col % 32) // 16, (row % 32) // 2 == col % 16
+    back = ((row % 32) // 16 == (col // 32) // 2) & (row % 16 == (col % 32) // 2)
+    one = lambda where, value: jnp.where(where, value, 0.0).astype(jnp.bfloat16)
+    r["to_1"][...] = shrink_lanes(256, 128)
+    r["to_2"][...] = shrink_lanes(128, 64)
+    r["to_3"][...] = one((row < 64) & (row // 2 == col % 32), 0.125)
+    r["to_4"][...] = one(same_x & same_z, 0.125)
+    r["from_4"][...] = one(back, 1.0)
+    r["from_3"][...] = one(row % 32 == (col % 64) // 2, 1.0)
+    r["from_2"][...] = grow_lanes(64, 128)
+    r["from_1"][...] = grow_lanes(128, 256)
+
     for copy in loads_k:
         copy.wait()
     turn(r["k_in"], r["k0"])
@@ -669,18 +683,16 @@
 
     half, sums, doubled = r["half"], r["sums"], r["doubled"]
     k0, k1, k2 = r["k0"], r["k1"], r["k2"]
-    to_1, to_2 = shrink_lanes(256, 128), shrink_lanes(128, 64)
+    to_1, to_2 = r["to_1"], r["to_2"]
     restrict(lambda p: k0[p, 0 : l0.x, :], k1, l1.n, l0.h, l1.h, l0.x, to_1, half, sums)
     l1.k.start(place)
     restrict(lambda p: k1[p, 0 : l1.x, :], k2, l2.n, l1.h, l2.h, l1.x, to_2, half, sums)
 
     def small_block(read):
-        row, col = iota((128, 128), 0), iota((128, 128), 1)
-        matrix = jnp.where((row < 64) & (row // 2 == col % 32), 0.125, 0.0).astype(jnp.bfloat16)
         tile = (8, 128)
         mine = iota(tile, 1) // 32 == iota(tile, 0) // 2
         pairs = [read(l2.h + 2 * j) + read(l2.h + 2 * j + 1) for j in range(2)]
-        means = times(jnp.concatenate(pairs, axis=0), matrix)
+        means = times(jnp.concatenate(pairs, axis=0), r["to_3"][...])
         found = jnp.zeros(tile, F32)
         for j in range(2):
             spread = jnp.where(mine, means[8 * j : 8 * j + 8], 0.0)
@@ -812,30 +824,28 @@
         count, fine = below.n + 2 * margin, level.h - 2 * margin
         restrict(read, target, count, fine, below.h - margin, rows, matrix, half, sums)
 
-    ready(l0, gather_k.along_z)
+    ready(l0)
     descend(l0, sources[0], 2)
-    source_below(l0, r["b1"], 0, l0.x, shrink_lanes(256, 128))
+    source_below(l0, r["b1"], 0, l0.x, to_1)
     sources[1].start(place)
-    gather_k.along_gx()
+    gather_k.along_z()
     l2.k.start(place)
     ready(l1)
-    descend(l1, sources[1], 6)
-    source_below(l1, r["b2"], 2, l1.x + 16, shrink_lanes(128, 64))
+    sources[1].arrive(range(8))
+    gather_k.along_gx()
+    descend(l1, None, 6)
+    source_below(l1, r["b2"], 2, l1.x + 16, to_2)
     ready(l2)
     descend(l2, None, 2)
     gather_b.along_x(small_block(lambda p: l2.residual(l2.x2, p)[0 : l2.x, :]))
     def to_bottom(source, low):
-        row, col = iota((128, 128), 0), iota((128, 128), 1)
-        same_x = (row // 32) // 2 == (col % 32) // 16
-        same_z = (row % 32) // 2 == col % 16
-        matrix = jnp.where(same_x & same_z, 0.125, 0.0).astype(jnp.bfloat16)
         kept = 4 * ring_z
         pieces = []
         for g in range(count_x):
             even = source[g, pl.ds(low, kept, stride=2), :]
             odd = source[g, pl.ds(low + 1, kept, stride=2), :]
             pieces.append(even + odd)
-        means = times(jnp.concatenate(pieces, axis=0), matrix)
+        means = times(jnp.concatenate(pieces, axis=0), r["to_4"][...])
         group = iota((8, 128), 1) // 32
         tiles = []
         for g in range(count_x):
@@ -864,12 +874,9 @@
     for g in range(count_x):
         tiles4[g + 1] = deepest[g]
 
-    row, col = iota((128, 128), 0), iota((128, 128), 1)
-    same = ((row % 32) // 16 == (col // 32) // 2) & (row % 16 == (col % 32) // 2)
-    matrix_43 = jnp.where(same, 1.0, 0.0).astype(jnp.bfloat16)
     group = iota((8, 128), 1) // 32
     spread = [jnp.where(group == q, tiles4[gx + c], 0.0) for c in range(3) for q in range(4)]
-    wide = times(jnp.concatenate(spread, axis=0), matrix_43)
+    wide = times(jnp.concatenate(spread, axis=0), r["from_4"][...])
     for c in range(3):
         piece = wide[32 * c : 32 * c + 32]
         grown3[c, pl.ds(LOW, 32, stride=2), :] = piece
@@ -878,7 +885,6 @@
     answer = r["answer"]
     l3.up(gx, pl.multiple_of(start, 8), grown3, (z0_3, z1_3), answer)
 
-    matrix_32 = jnp.where(iota((128, 128), 0) % 32 == (iota((128, 128), 1) % 64) // 2, 1.0, 0.0).astype(jnp.bfloat16)
     l2.xh.arrive(range(8))
     l2.xh.merge(0, 2 * l2.h + l2.n)
     tile = (8, 128)
@@ -890,7 +896,7 @@
         lower, own, upper = [jnp.broadcast_to(answer[c, pl.ds(at, 1), :], tile) for c in range(3)]
         spread.append(jnp.where(own_group, own, 0.0))
         spread.append(jnp.where(own_group, jnp.where(first_half, upper, lower), 0.0))
-    wide = times(jnp.concatenate(spread, axis=0), matrix_32)
+    wide = times(jnp.concatenate(spread, axis=0), r["from_3"][...])
     l2.rows_ok = l2.row_ok()
     low_lanes = iota(l2.shape, 1) < 64
     for p in range(12):
@@ -902,7 +908,7 @@
     l2.third(1, 11)
     l2.fourth(2, 10, r["z2"])
 
-    grow(r["z2"], (2, 10), 16, grow_lanes(64, 128), doubled)
+    grow(r["z2"], (2, 10), 16, r["from_2"], doubled)
     l1.rows_ok = l1.row_ok()
 
     def lift_1(j):
@@ -914,7 +920,7 @@
     l1.third(l1.h - 3, l1.h + l1.n + 3)
     l1.fourth(l1.h - 2, l1.h + l1.n + 2, r["z1out"])
 
-    grow(r["z1out"], (l1.h - 2, l1.h + l1.n + 2), 32, grow_lanes(128, 256), doubled)
+    grow(r["z1out"], (l1.h - 2, l1.h + l1.n + 2), 32, r["from_1"], doubled)
     l0.xh.arrive(range(8))
     l0.xh.merge(l0.h - 2, l0.h + l0.n + 2)
     l0.rows_ok = l0.row_ok()
@@ -965,6 +971,8 @@
         "load": pltpu.SemaphoreType.DMA((8,)),
         "half": vmem(2, 2, nx, 128),
         "idle": vmem(256, 8, 128),
+        "to_1": pltpu.VMEM((256, 128), jnp.bfloat16),
+        "from_1": pltpu.VMEM((128, 256), jnp.bfloat16),
         "sums": vmem(nx * ny // 4, nz),
         "doubled": vmem(ny // 2 + 4, 2, nx + 32, 128),
         "z0_3": vmem(5, 24, 128),
@@ -978,6 +986,8 @@
         "z2": vmem((ny >> 2) + 8, (nx >> 2) + 8, 128),
         "z1out": vmem((ny >> 1) + 14, (nx >> 1) + 16, 128),
     }
+    for name in ("to_2", "to_3", "to_4", "from_4", "from_3", "from_2"):
+        scratch[name] = pltpu.VMEM((128, 128), jnp.bfloat16)
     for number, (lanes, halo, *depths) in enumerate(SHAPES):
         rows, planes, width = nx >> number, ny >> number, max(128, lanes)
         wide = number == 1

time: 55.8 us -> 54.6 us (0.978)
  Pallas kernels: 52.3 us -> 51.1 us
    pallas_call x1, Pallas kernels: 52.3 us -> 51.1 us  [per_device(): pl.pallas_call(functools.partial(kernel, count_x, count_y, names), out_sh...]
where the time goes in v5:
time: 54.6 us; the launch traced here: 54.4 us
  Pallas kernels  51.1 us (94%)
  local copies, waits for them, and re-layouts  2.72 us (5%)
  between operations  0.65 us (1%)
    pallas_call x1, Pallas kernels, per_device(): pl.pallas_call(functools.partial(kernel, count_x, count_y, names), out_sh...  51.1 us
    unnamed x4, local copies, waits for them, and re-layouts  2.72 us

profile of v5, /device:TPU:1, one launch (start us, length us, event | category | flops | bytes accessed | tf_op | source)
XLA Modules:
  0.0 54.4 jit_solution(1990001449587193590)
XLA Ops:
  0.6 51.1 %vcycle.1 = (f32[512,256]{1,0:T(8,128)}, f32[512,256]{1,0:T(8,128)}) custom-call(f32[512,256]{1,0:T(8,128)} %bitcast.4, f32[512,256]{1,0:T(8,128)} %bitcast.5), custom_call_target="tpu_custom_call" | custom-call | tf_op jit(solution)/shard_map/vcycle/pallas_call | solution.py:1017
  51.7 0.0 copy-start
  51.7 1.9 %copy.6 = f32[32,16,256]{2,1,0:T(8,128)} copy(f32[32,16,256]{2,1,0:T(8,128)} %bitcast.7) | data formatting | bytes 1048576
  53.6 0.0 copy-done
  53.6 0.8 %copy.7 = f32[32,16,256]{2,1,0:T(8,128)} copy(f32[32,16,256]{2,1,0:T(8,128)S(1)} %bitcast.6) | data formatting | bytes 1048576
Async XLA Ops:
  51.7 1.9 %copy-start = (f32[512,256]{1,0:T(8,128)S(1)}, f32[512,256]{1,0:T(8,128)}, u32[]{:S(2)}) copy-start(f32[512,256]{1,0:T(8,128)} %get-tuple-element.5) | copy-start | bytes 1572868

commit v6 on v5

--- a/solution.py
+++ b/solution.py
@@ -388,7 +388,7 @@
             last = lane % self.size_z == self.size_z - 1
             self.wz[g, inside, :] = jnp.where(last, 0.0, harmonic(own, roll(own, -1, 1)))
 
-        loop(1, self.count + 1, faces)
+        loop(1, self.count + 1, faces, 2)
 
         def totals(g):
             lane, row = iota(self.shape, 1), iota(self.shape, 0)
@@ -404,7 +404,7 @@
             self.w[g, inside, :] = total
             self.inv[g, inside, :] = 1.0 / total
 
-        loop(1, self.count + 1, totals)
+        loop(1, self.count + 1, totals, 2)
 
     def flow(self, fields, weights):
         previous, own, following = fields
@@ -425,20 +425,20 @@
             found = self.at(self.b, g) * self.at(self.inv, g) * (1.0 / (THETA * self.scale))
             self.x1[g, inside, :] = found
 
-        loop(1, self.count + 1, first, 2)
+        loop(1, self.count + 1, first, 8)
 
         def second(g):
             factor = 1.0 + MOMENTUM + STEP * (THETA - 1.0)
             moved = self.at(self.inv, g) * self.beside(self.x1, g)
             self.x2[g, inside, :] = factor * self.at(self.x1, g) + STEP * moved
 
-        loop(1, self.count + 1, second, 2)
+        loop(1, self.count + 1, second, 8)
 
         def residual(g):
             applied = self.at(self.w, g) * self.at(self.x2, g) - self.beside(self.x2, g)
             left[g - 1] = self.at(self.b, g) - self.scale * applied
 
-        loop(1, self.count + 1, residual, 2)
+        loop(1, self.count + 1, residual, 8)
 
     def up(self, gx, start, grown, held, answer):
         span = pl.ds(start, 24)
@@ -674,11 +674,11 @@
     for copy in loads_k:
         copy.wait()
     turn(r["k_in"], r["k0"])
+    pl.semaphore_wait(barrier, len(partners))
+    l0.k.start(place)
     for copy in loads_b:
         copy.wait()
     turn(r["b_in"], r["b0"])
-    pl.semaphore_wait(barrier, len(partners))
-    l0.k.start(place)
     sources[0].start(place)
 
     half, sums, doubled = r["half"], r["sums"], r["doubled"]

time: 54.6 us -> 54 us (0.989)
  Pallas kernels: 51.1 us -> 50.5 us
where the time goes in v6:
time: 54 us; the launch traced here: 53.9 us
  Pallas kernels  50.5 us (94%)
  local copies, waits for them, and re-layouts  2.72 us (5%)
  between operations  0.65 us (1%)
    pallas_call x1, Pallas kernels, per_device(): pl.pallas_call(functools.partial(kernel, count_x, count_y, names), out_sh...  50.5 us
    unnamed x4, local copies, waits for them, and re-layouts  2.72 us

profile of v6, /device:TPU:1, one launch (start us, length us, event | category | flops | bytes accessed | tf_op | source)
XLA Modules:
  0.0 53.9 jit_solution(5618291895321570909)
XLA Ops:
  0.6 50.5 %vcycle.1 = (f32[512,256]{1,0:T(8,128)}, f32[512,256]{1,0:T(8,128)}) custom-call(f32[512,256]{1,0:T(8,128)} %bitcast.4, f32[512,256]{1,0:T(8,128)} %bitcast.5), custom_call_target="tpu_custom_call" | custom-call | tf_op jit(solution)/shard_map/vcycle/pallas_call | solution.py:1017
  51.2 0.0 copy-start
  51.2 1.9 %copy.6 = f32[32,16,256]{2,1,0:T(8,128)} copy(f32[32,16,256]{2,1,0:T(8,128)} %bitcast.7) | data formatting | bytes 1048576
  53.1 0.0 copy-done
  53.1 0.8 %copy.7 = f32[32,16,256]{2,1,0:T(8,128)} copy(f32[32,16,256]{2,1,0:T(8,128)S(1)} %bitcast.6) | data formatting | bytes 1048576
Async XLA Ops:
  51.2 1.9 %copy-start = (f32[512,256]{1,0:T(8,128)S(1)}, f32[512,256]{1,0:T(8,128)}, u32[]{:S(2)}) copy-start(f32[512,256]{1,0:T(8,128)} %get-tuple-element.5) | copy-start | bytes 1572868

commit v7 on v6

--- a/solution.py
+++ b/solution.py
@@ -176,7 +176,7 @@
         self.x = self.k.rows
         self.shape = self.k.field.shape[1:]
         self.period = lanes
-        self.unroll = 2 if number == 0 else 4
+        self.unroll = 2 if number == 0 else 8
 
     def merge_k(self, start, stop):
         at_low = jnp.where(self.gx == 0, 1, 0)

time: 54 us -> 53.1 us (0.983)
  Pallas kernels: 50.5 us -> 49.6 us
    pallas_call x1, Pallas kernels: 50.5 us -> 49.6 us  [per_device(): pl.pallas_call(functools.partial(kernel, count_x, count_y, names), out_sh...]
where the time goes in v7:
time: 53.1 us; the launch traced here: 52.9 us
  Pallas kernels  49.6 us (93%)
  local copies, waits for them, and re-layouts  2.72 us (5%)
  between operations  0.65 us (1%)
    pallas_call x1, Pallas kernels, per_device(): pl.pallas_call(functools.partial(kernel, count_x, count_y, names), out_sh...  49.6 us
    unnamed x4, local copies, waits for them, and re-layouts  2.72 us

profile of v7, /device:TPU:1, one launch (start us, length us, event | category | flops | bytes accessed | tf_op | source)
XLA Modules:
  0.0 52.9 jit_solution(9676743977157264634)
XLA Ops:
  0.6 49.6 %vcycle.1 = (f32[512,256]{1,0:T(8,128)}, f32[512,256]{1,0:T(8,128)}) custom-call(f32[512,256]{1,0:T(8,128)} %bitcast.4, f32[512,256]{1,0:T(8,128)} %bitcast.5), custom_call_target="tpu_custom_call" | custom-call | tf_op jit(solution)/shard_map/vcycle/pallas_call | solution.py:1017
  50.2 0.0 copy-start
  50.2 1.9 %copy.6 = f32[32,16,256]{2,1,0:T(8,128)} copy(f32[32,16,256]{2,1,0:T(8,128)} %bitcast.7) | data formatting | bytes 1048576
  52.1 0.0 copy-done
  52.1 0.8 %copy.7 = f32[32,16,256]{2,1,0:T(8,128)} copy(f32[32,16,256]{2,1,0:T(8,128)S(1)} %bitcast.6) | data formatting | bytes 1048576
Async XLA Ops:
  50.2 1.9 %copy-start = (f32[512,256]{1,0:T(8,128)S(1)}, f32[512,256]{1,0:T(8,128)}, u32[]{:S(2)}) copy-start(f32[512,256]{1,0:T(8,128)} %get-tuple-element.5) | copy-start | bytes 1572868
